TPU v7x, 32 devices: a whole 2x2x4 slice. The times are simulated.
32 devices in a mesh: seq: 16 (over z, y, x), head: 2 (over core).
Axes of the slice: x: 2, y: 2, z: 4, core: 2. Of those that a mesh axis runs over, the one named last changes fastest.
Arguments:
- queries: bfloat16 [128, 1024], P(None, 'head'), may hold values from -400 to 400
- keys: bfloat16 [4096, 256], P('seq', 'head'), may hold values from -6 to 6
- values: bfloat16 [4096, 256], P('seq', 'head'), may hold values from -6 to 6
- householder: bfloat16 [4096, 256], P('seq', 'head'), may hold values from -6 to 6
- out_proj: bfloat16 [1024, 1024], P('head', 'seq'), may hold values from -0.1875 to 0.1875
Outputs:
- mixed: bfloat16 [128, 1024], P('head', 'seq')
All inputs are finite; a program needn't handle non-finite values.
Results may differ from a plain program's by a relative error of at most 0.02.
Values may be sent and summed in bfloat16 or wider, within the bound.
No kernel may reach another device: no remote copies, remote signals or barrier semaphores. Data moves between devices by JAX's collectives and lax.ppermute only.
A program may use at most 64 MiB of HBM per device.

v0:
```python
import jax
import jax.numpy as jnp
from jax import lax
from jax.sharding import PartitionSpec as P

BLOCK = 64


def unit_rows(raw_vecs):
    return raw_vecs * lax.rsqrt(jnp.sum(raw_vecs * raw_vecs, axis=-1, keepdims=True) + 1e-06)


def span_forms(raw_vecs, keys_float):
    precise = lax.Precision.HIGHEST
    vectors = unit_rows(raw_vecs)
    block_len = vectors.shape[1]
    head_width = vectors.shape[2]
    row_ids = lax.broadcasted_iota(jnp.int32, (block_len, block_len), 0)
    col_ids = lax.broadcasted_iota(jnp.int32, (block_len, block_len), 1)
    gram = jnp.einsum("nad,nbd->nab", vectors, vectors, precision=precise)
    lower = jnp.where(row_ids > col_ids, gram, 0.0) + jnp.where(row_ids == col_ids, 0.5, 0.0)
    identity_block = jnp.broadcast_to(jnp.eye(block_len, dtype=jnp.float32), lower.shape)
    coeff = jax.scipy.linalg.solve_triangular(lower, identity_block, lower=True)
    identity_head = jnp.eye(head_width, dtype=jnp.float32)
    transition = identity_head - jnp.einsum(
        "nad,nab,nbe->nde", vectors, coeff, vectors, precision=precise
    )
    inner = jnp.einsum("nbd,njd->nbj", vectors, keys_float, precision=precise)
    inner = jnp.where(row_ids > col_ids, inner, 0.0)
    mixing = jnp.einsum("nab,nbj->naj", coeff, inner, precision=precise)
    carried = keys_float - jnp.einsum("naj,nad->njd", mixing, vectors, precision=precise)
    return (transition, carried)


def carry_back(transition, carried, identity_head):
    precise = lax.Precision.HIGHEST

    def advance(running, span_item):
        factor, block_keys = span_item
        emitted = jnp.dot(block_keys, running.T, precision=precise)
        return (jnp.dot(running, factor, precision=precise), emitted)

    return lax.scan(advance, identity_head, (transition, carried), reverse=True)


def compose_batch(earlier, later):
    return jnp.einsum("nab,nbc->nac", earlier, later, precision=lax.Precision.HIGHEST)


def on_device(queries, keys, values, householder, out_proj):
    precise = lax.Precision.HIGHEST
    ctx_rows, head_width = keys.shape
    blocks = ctx_rows // BLOCK
    raw_vecs = householder.astype(jnp.float32).reshape(blocks, BLOCK, head_width)
    keys_float = keys.astype(jnp.float32).reshape(blocks, BLOCK, head_width)
    transition, carried = span_forms(raw_vecs, keys_float)
    identity_head = jnp.eye(head_width, dtype=jnp.float32)
    shard_mat, local_keys = carry_back(transition, carried, identity_head)
    local_keys = local_keys.reshape(ctx_rows, head_width)
    all_trans = lax.all_gather(shard_mat[None], "seq", axis=0, tiled=True)
    my_index = lax.axis_index("seq")
    inclusive = lax.associative_scan(compose_batch, all_trans, reverse=True)
    padded_stack = jnp.concatenate([inclusive, identity_head[None]], axis=0)
    suffix_mat = lax.dynamic_index_in_dim(padded_stack, my_index + 1, 0, keepdims=False)
    query_count = queries.shape[0]
    group_size = queries.shape[1] // head_width
    query_float = queries.astype(jnp.float32).reshape(query_count, group_size, head_width)
    turned = jnp.einsum("ihe,ef->hif", query_float, suffix_mat, precision=precise)
    inv_root = 1.0 / jnp.sqrt(jnp.float32(head_width))

    def attend(query_rows):
        scores = jnp.einsum("if,jf->ij", query_rows, local_keys, precision=precise) * inv_root
        peak = jnp.max(scores, axis=1)
        expo = jnp.exp(scores - peak[:, None])
        totals = jnp.sum(expo, axis=1)
        numerators = jnp.dot(expo.astype(jnp.bfloat16), values, preferred_element_type=jnp.float32)
        return (peak, totals, numerators)

    peaks, totals, numerators = lax.map(attend, turned)
    peak_all, total_all, numer_all = (
        lax.all_to_all(peaks[None], "seq", split_axis=2, concat_axis=0, tiled=True),
        lax.all_to_all(totals[None], "seq", split_axis=2, concat_axis=0, tiled=True),
        lax.all_to_all(numerators[None], "seq", split_axis=2, concat_axis=0, tiled=True),
    )
    best = jnp.max(peak_all, axis=0)
    factors = jnp.exp(peak_all - best[None])
    merged_total = jnp.sum(factors * total_all, axis=0)
    merged_numer = jnp.sum(factors[..., None] * numer_all, axis=0)
    own_rows = (merged_numer / merged_total[..., None]).astype(jnp.bfloat16)
    attention = lax.all_gather(own_rows, "seq", axis=1, tiled=True)
    flat_attention = jnp.transpose(attention, (1, 0, 2)).reshape(
        query_count, group_size * head_width
    )
    return lax.psum_scatter(
        jnp.dot(flat_attention, out_proj, preferred_element_type=jnp.float32).astype(jnp.bfloat16),
        "head",
        scatter_dimension=0,
        tiled=True,
    )


def solution(mesh):
    placed = (
        P(None, "head"),
        P("seq", "head"),
        P("seq", "head"),
        P("seq", "head"),
        P("head", "seq"),
    )
    return jax.shard_map(
        on_device, mesh=mesh, in_specs=placed, out_specs=P("head", "seq"), check_vma=False
    )
```

profile of v0, /device:TPU:0, one launch (start us, length us, event | category | flops | bytes accessed | tf_op | source)
XLA Modules:
  0.0 198.7 jit_solution(75393029782311730)
XLA Ops:
  6.6 1.0 multiply_reduce_fusion
  7.7 1.3 fusion.17
  9.0 19.7 %custom-call.4 = f32[4,1,64,64]{2,3,1,0:T(8,128)S(1)} custom-call(f32[4,1,64,64]{3,2,1,0:T(8,128)S(1)} %fusion.17), custom_call_target="InvertDiagBlocksLowerTriangular" | custom-call | tf_op jit(solution)/shard_map/jit(_solve_triangular)/vmap()/triangular_solve | solution.py:23
  28.7 1.2 convolution_select_fusion
  29.9 0.4 fusion.30
  30.3 0.4 fusion.38
  30.7 0.4 fusion.71
  31.1 0.3 convolution_subtract_fusion.1
  31.6 0.7 convolution_subtract_fusion
  32.3 2.1 %while.30 = (s32[]{:T(128)}, f32[128,128]{0,1:T(8,128)S(1)}, f32[4,64,128]{2,1,0:T(8,128)S(1)}, f32[4,128,128]{2,1,0:T(8,128)S(1)}, f32[4,64,128]{2,1,0:T(8,128)S(1)}, /*index=5*/s32[]{:T(128)}, s32[]{:T(128)}) while((s32[]{:T(128)}, f32[128,128]{0,1:T(8,128)S(1)}, f32[4,64,128]{2,1,0:T(8,128)S(1)}, f32[4,128,128]{2,1,0:T(8,128)S(1)}, ...), condition=%wide.region_2.3_spmd, body=%wide.region_1.2_spmd.sunk | while | flops 37748736 | bytes 459869 | solution.py:43
  32.5 0.3 convolution_bitcast_fusion.6
  33.0 0.3 convolution_bitcast_fusion.6
  33.5 0.3 convolution_bitcast_fusion.6
  34.1 0.3 convolution_bitcast_fusion.6
  34.4 0.7 copy.21
  35.2 57.9 %all-gather.3.cloned.1.call-done = f32[2048,128]{1,0:T(8,128)} async-done(((f32[128,128]{1,0:T(8,128)}), f32[2048,128]{1,0:T(8,128)}) %all-gather.3.cloned.1.call-update) | async-done | bytes 1048592 | tf_op jit(solution)/shard_map/all_gather | solution.py:60
  93.1 1.2 slice.72
  94.5 0.6 fusion.18
  95.1 0.4 fusion.23
  95.5 0.3 fusion.32
  95.8 0.2 convolution_bitcast_fusion.4
  96.0 0.2 convolution_bitcast_fusion.3
  96.4 0.3 fusion.26
  97.0 0.6 fusion.20
  98.2 0.3 convolution_bitcast_fusion.2
  98.5 0.5 copy-done.2
  99.0 15.2 %while.31 = (s32[]{:T(128)}, f32[4,128]{1,0:T(4,128)S(1)}, f32[4,128]{1,0:T(4,128)S(1)}, f32[4,128,128]{2,0,1:T(4,128)}, f32[4,128,128]{1,2,0:T(8,128)S(1)}, /*i...) while((s32[]{:T(128)}, f32[4,128]{1,0:T(4,128)S(1)}, ...), condition=%wide.region_6.7_spmd, body=%wide.region_3.6_spmd.sunk | while | flops 58916608 | bytes 856173 | solution.py:79
  99.0 0.4 fusion.107
  99.4 0.2 fusion.109
  99.6 2.9 %dynamic_update_slice.29 = f32[4,128,128]{2,0,1:T(4,128)} dynamic-update-slice(f32[4,128,128]{2,0,1:T(4,128)} %get-tuple-element.315, f32[1,128,128]{2,0,1:T(1,128)S(1)} %bitcast.133, s32[]{:T(128)} %get-tuple-element.312, s32[]{:T(128)} %constant.80.clone.1..sunk, s32[]{:T(128)} %constant.80.clone.1..sunk) | dynamic-update-slice | bytes 131076 | tf_op jit(solution)/shard_map/while/body/jit(dynamic_update_index_in_dim)/dynamic_update_slice | solution.py:79
  102.8 0.4 fusion.107
  103.2 0.2 fusion.109
  103.4 2.9 %dynamic_update_slice.29 = f32[4,128,128]{2,0,1:T(4,128)} dynamic-update-slice(f32[4,128,128]{2,0,1:T(4,128)} %get-tuple-element.315, f32[1,128,128]{2,0,1:T(1,128)S(1)} %bitcast.133, s32[]{:T(128)} %get-tuple-element.312, s32[]{:T(128)} %constant.80.clone.1..sunk, s32[]{:T(128)} %constant.80.clone.1..sunk) | dynamic-update-slice | bytes 131076 | tf_op jit(solution)/shard_map/while/body/jit(dynamic_update_index_in_dim)/dynamic_update_slice | solution.py:79
  106.6 0.4 fusion.107
  107.0 0.2 fusion.109
  107.2 2.9 %dynamic_update_slice.29 = f32[4,128,128]{2,0,1:T(4,128)} dynamic-update-slice(f32[4,128,128]{2,0,1:T(4,128)} %get-tuple-element.315, f32[1,128,128]{2,0,1:T(1,128)S(1)} %bitcast.133, s32[]{:T(128)} %get-tuple-element.312, s32[]{:T(128)} %constant.80.clone.1..sunk, s32[]{:T(128)} %constant.80.clone.1..sunk) | dynamic-update-slice | bytes 131076 | tf_op jit(solution)/shard_map/while/body/jit(dynamic_update_index_in_dim)/dynamic_update_slice | solution.py:79
  110.4 0.4 fusion.107
  110.8 0.2 fusion.109
  111.0 2.9 %dynamic_update_slice.29 = f32[4,128,128]{2,0,1:T(4,128)} dynamic-update-slice(f32[4,128,128]{2,0,1:T(4,128)} %get-tuple-element.315, f32[1,128,128]{2,0,1:T(1,128)S(1)} %bitcast.133, s32[]{:T(128)} %get-tuple-element.312, s32[]{:T(128)} %constant.80.clone.1..sunk, s32[]{:T(128)} %constant.80.clone.1..sunk) | dynamic-update-slice | bytes 131076 | tf_op jit(solution)/shard_map/while/body/jit(dynamic_update_index_in_dim)/dynamic_update_slice | solution.py:79
  114.2 0.7 copy.25
  114.9 4.5 %all-to-all-start = ((f32[1,4,128]{1,0,2:T(1,128)}), f32[1,4,128]{1,0,2:T(1,128)S(1)}, u32[]{:S(2)}, u32[]{:S(2)}) async-start(f32[1,4,128]{1,0,2:T(1,128)} %bitcast.24), calls=%async_computation | async-start | bytes 131072 | tf_op jit(solution)/shard_map/all_to_all | solution.py:81
  119.5 7.4 %all-to-all-done = f32[1,4,128]{1,0,2:T(1,128)S(1)} async-done(((f32[1,4,128]{1,0,2:T(1,128)}), f32[1,4,128]{1,0,2:T(1,128)S(1)}, u32[]{:S(2)}, u32[]{:S(2)}) %all-to-all-start) | async-done | bytes 2080 | tf_op jit(solution)/shard_map/all_to_all | solution.py:81
  126.9 10.1 %all_to_all.54 = f32[1,4,128]{1,0,2:T(1,128)S(1)} all-to-all(f32[1,4,128]{1,0,2:T(1,128)S(1)} %bitcast.147), channel_id=1, replica_groups=mesh['seq'=16,'head'=2] {'seq'}, dimensions={2} | all-to-all | bytes 4096 | tf_op jit(solution)/shard_map/all_to_all | solution.py:82
  137.0 3.5 %all-to-all-start.1 = ((f32[1,4,128,128]{3,1,0,2:T(4,128)}), f32[1,4,128,128]{3,1,0,2:T(4,128)S(1)}, u32[]{:S(2)}, u32[]{:S(2)}) async-start(f32[1,4,128,128]{3,1,0,2:T(4,128)} %bitcast.28), calls=%async_computation.1 | async-start | bytes 524288 | tf_op jit(solution)/shard_map/all_to_all | solution.py:83
  141.0 8.0 %all-to-all-done.1 = f32[1,4,128,128]{3,1,0,2:T(4,128)S(1)} async-done(((f32[1,4,128,128]{3,1,0,2:T(4,128)}), f32[1,4,128,128]{3,1,0,2:T(4,128)S(1)}, u32[]{:S(2)}, u32[]{:S(2)}) %all-to-all-start.1) | async-done | bytes 262176 | tf_op jit(solution)/shard_map/all_to_all | solution.py:83
  149.3 38.1 %all_gather.7 = bf16[4,128,128]{2,0,1:T(4,128)(2,1)S(1)} all-gather(bf16[4,8,128]{2,0,1:T(4,128)(2,1)S(1)} %copy.31), channel_id=1, replica_groups=mesh['seq'=16,'head'=2] {'seq'}, dimensions={1}, use_global_device_ids=true | all-gather | bytes 139264 | tf_op jit(solution)/shard_map/all_gather | solution.py:90
  187.5 0.8 convolution_convert_fusion
  188.4 3.5 %reduce-scatter.2.cloned.1.call-done = bf16[64,64]{1,0:T(8,128)(2,1)} async-done(((bf16[128,64]{1,0:T(8,128)(2,1)}), bf16[64,64]{1,0:T(8,128)(2,1)}) %reduce-scatter.2.cloned.1.call-update) | async-done | bytes 8208 | tf_op jit(solution)/shard_map/reduce_scatter | solution.py:94
  (75 shorter events, 4.0 us)
Async XLA Ops:
  6.5 91.6 %copy-start = (bf16[128,512]{1,0:T(8,128)(2,1)S(1)}, bf16[128,512]{1,0:T(8,128)(2,1)}, u32[]{:S(2)}) copy-start(bf16[128,512]{1,0:T(8,128)(2,1)} %param.9) | copy-start | bytes 393220
  6.5 23.7 %copy-start.1 = (bf16[256,128]{1,0:T(8,128)(2,1)S(1)}, bf16[256,128]{1,0:T(8,128)(2,1)}, u32[]{:S(2)}) copy-start(bf16[256,128]{1,0:T(8,128)(2,1)} %param.12) | copy-start | bytes 196612
  6.5 24.6 %copy-start.4 = (bf16[256,128]{1,0:T(8,128)(2,1)S(1)}, bf16[256,128]{1,0:T(8,128)(2,1)}, u32[]{:S(2)}) copy-start(bf16[256,128]{1,0:T(8,128)(2,1)} %param.10) | copy-start | bytes 196612
  6.5 86.5 %all-gather.3.cloned.1.call-start = ((), (), s32[]{:S(2)}) async-start(), calls=%async_computation.5 | async-start | bytes 1114112 | tf_op jit(solution)/shard_map/all_gather | solution.py:60
  93.1 1.4 copy-start.3
  98.1 0.8 copy-start.2
  114.2 73.3 %copy-start.5 = (bf16[512,64]{0,1:T(8,128)(2,1)S(1)}, bf16[512,64]{0,1:T(8,128)(2,1)}, u32[]{:S(2)}) copy-start(bf16[512,64]{0,1:T(8,128)(2,1)} %param.13) | copy-start | bytes 196612
  114.9 12.0 %all-to-all-start = ((f32[1,4,128]{1,0,2:T(1,128)}), f32[1,4,128]{1,0,2:T(1,128)S(1)}, u32[]{:S(2)}, u32[]{:S(2)}) async-start(f32[1,4,128]{1,0,2:T(1,128)} %bitcast.24), calls=%async_computation | async-start | bytes 131072 | tf_op jit(solution)/shard_map/all_to_all | solution.py:81
  137.0 12.0 %all-to-all-start.1 = ((f32[1,4,128,128]{3,1,0,2:T(4,128)}), f32[1,4,128,128]{3,1,0,2:T(4,128)S(1)}, u32[]{:S(2)}, u32[]{:S(2)}) async-start(f32[1,4,128,128]{3,1,0,2:T(4,128)} %bitcast.28), calls=%async_computation.1 | async-start | bytes 524288 | tf_op jit(solution)/shard_map/all_to_all | solution.py:83
  140.6 51.3 %reduce-scatter.2.cloned.1.call-start = ((), (), s32[]{:S(2)}) async-start(), calls=%async_computation.4 | async-start | bytes 49152 | tf_op jit(solution)/shard_map/reduce_scatter | solution.py:94
Sparse Core Ops, SparseCore 0:
  35.2 57.7 all-gather.2
  188.5 3.3 reduce-scatter.1
where the time goes:
time: 199 us
  waiting for transfers between devices  76.9 us (39%)
  blocking collectives  48.2 us (24%)
  other arithmetic  22 us (11%)
  local copies, waits for them, and re-layouts  16.7 us (8%)
  between operations  13.9 us (7%)
  matrix products  12.9 us (6%)
  starting transfers between devices  8.03 us (4%)
    all_gather x1, waiting for transfers between devices, on_device(): all_trans = lax.all_gather(shard_mat[None], 'seq', axis=0, tiled=True)  57.9 us
    all_gather x1, blocking collectives, on_device(): attention = lax.all_gather(own_rows, 'seq', axis=1, tiled=True)  38.1 us
    another operation x1, other arithmetic, span_forms(): coeff = jax.scipy.linalg.solve_triangular(lower, identity_block, lower=True)  19.7 us
    dynamic_update_slice x12, local copies, waits for them, and re-layouts, on_device(): peaks, totals, numerators = lax.map(attend, turned)  12 us
    all_to_all x1, blocking collectives, on_device(): lax.all_to_all(totals[None], 'seq', split_axis=2, concat_axis=0, tiled=True)  10.1 us
    all_to_all x1, waiting for transfers between devices, on_device(): lax.all_to_all(numerators[None], 'seq', split_axis=2, concat_axis=0, tile...  8.01 us
    all_to_all x1, waiting for transfers between devices, on_device(): lax.all_to_all(peaks[None], 'seq', split_axis=2, concat_axis=0, tiled=True)  7.42 us
    all_to_all x1, starting transfers between devices, on_device(): lax.all_to_all(peaks[None], 'seq', split_axis=2, concat_axis=0, tiled=True)  4.45 us
  transfers between devices with their start and end apart: 4, of which 4 were waited for; matrix products, arithmetic and copies ran while one was open for 0% of the time, Pallas kernels for 0%

commit v1 on v0

v1 whole, which is shorter than its diff:
```python
import functools

import jax
import jax.numpy as jnp
from jax import lax
from jax.experimental import pallas as pl
from jax.experimental.pallas import tpu as pltpu
from jax.sharding import PartitionSpec as P

BLOCK = 64
F32 = jnp.float32
BF16 = jnp.bfloat16
VMEM = pl.BlockSpec(memory_space=pltpu.VMEM)
SMEM = pl.BlockSpec(memory_space=pltpu.SMEM)


def mm(a, b):
    return lax.dot_general(
        a, b, (((1,), (0,)), ((), ())), precision=lax.Precision.HIGHEST, preferred_element_type=F32
    )


def mm_nt(a, b):
    return lax.dot_general(
        a, b, (((1,), (1,)), ((), ())), precision=lax.Precision.HIGHEST, preferred_element_type=F32
    )


def mm_fast(a, b):
    return lax.dot_general(a, b, (((1,), (0,)), ((), ())), preferred_element_type=F32)


def iotas(rows, cols):
    return (
        lax.broadcasted_iota(jnp.int32, (rows, cols), 0),
        lax.broadcasted_iota(jnp.int32, (rows, cols), 1),
    )


def eye(size):
    row, col = iotas(size, size)
    return jnp.where(row == col, 1.0, 0.0).astype(F32)


def chain(mats):
    mats = list(mats)
    while len(mats) > 1:
        mats = [
            mm(mats[i], mats[i + 1]) if i + 1 < len(mats) else mats[i]
            for i in range(0, len(mats), 2)
        ]
    return mats[0]


def call(kernel, outs, flops, **kw):
    single = not isinstance(outs, (tuple, list))
    many = (outs,) if single else tuple(outs)
    return pl.pallas_call(
        kernel,
        out_shape=outs if single else list(many),
        cost_estimate=pl.CostEstimate(flops=flops, bytes_accessed=1 << 20, transcendentals=0),
        **kw,
    )


def spans_kernel(raw_ref, total_ref, unit_ref, u_ref, parts_ref):
    raw = raw_ref[...].astype(F32)
    rows, width = raw.shape
    unit = raw * lax.rsqrt(jnp.sum(raw * raw, axis=-1, keepdims=True) + 1e-06)
    unit_ref[...] = unit
    turned = unit.T
    pair = 2 * BLOCK
    row, col = iotas(pair, pair)
    ident = eye(width)
    blocks = []
    for p in range(rows // pair):
        v = unit[p * pair : (p + 1) * pair]
        gram = mm_nt(v, v) * 2.0
        size = 1
        inv = jnp.where(row == col, 1.0, 0.0)
        while size < BLOCK:
            corner = (row // (2 * size) == col // (2 * size)) & (row // size < col // size)
            c = jnp.where(corner, gram, 0.0)
            if size == 1:
                inv = inv - c
            else:
                inv = inv - mm(inv, mm(c, inv))
            size *= 2
        u = mm(inv, v) * 2.0
        u_ref[p * pair : (p + 1) * pair, :] = u
        for b in range(2):
            lo = p * pair + b * BLOCK
            q = ident - mm(turned[:, lo : lo + BLOCK], u[b * BLOCK : (b + 1) * BLOCK])
            parts_ref[2 * p + b] = q
            blocks.append(q)
    total_ref[...] = chain(blocks)


def carry_kernel(half, keys_ref, unit_ref, u_ref, parts_ref, queries_ref, carried_ref, mixed_q_ref):
    keys = keys_ref[...].astype(F32)
    rows, width = keys.shape
    row, col = iotas(BLOCK, BLOCK)
    suffix = None
    for b in reversed(range(rows // BLOCK)):
        sl = slice(b * BLOCK, (b + 1) * BLOCK)
        k = keys[sl]
        inner = jnp.where(col > row, mm_nt(k, unit_ref[sl, :]), 0.0)
        done = k - mm(inner, u_ref[sl, :])
        carried_ref[sl, :] = done if suffix is None else mm(done, suffix)
        q = parts_ref[b]
        suffix = q if suffix is None else mm(q, suffix)
    mixed_q_ref[...] = reorder(half, queries_ref[...]).astype(BF16)


def reorder(half, x):
    halves, half_rows = half
    count = x.shape[0]
    row, col = iotas(count, count)
    group = halves * half_rows
    dest, rest = row // group, row % group
    source = (rest // half_rows) * (count // halves) + dest * half_rows + rest % half_rows
    return mm_fast(jnp.where(col == source, 1.0, 0.0).astype(BF16), x)


def sorted_slots(me, refs):
    vals = [r[...] for r in refs]
    slots = []
    for p in range(len(vals)):
        k = jnp.bitwise_xor(me, p)
        out = vals[0]
        for j in range(1, len(vals)):
            out = jnp.where(k == j, vals[j], out)
        slots.append(out)
    return slots


def digit(axis, stride, radix):
    return (lax.axis_index(axis) // stride) % radix


def total_kernel(stride, radix, *refs):
    *ins, out_ref = refs
    out_ref[...] = chain(sorted_slots(digit("seq", stride, radix), ins))


def later(me, slots):
    ident = eye(slots[0].shape[0])
    return [jnp.where(p > me, slots[p], ident) for p in range(1, len(slots))]


def shift_kernel(stride, radix, *refs):
    *ins, keys_ref, out_ref = refs
    me = digit("seq", stride, radix)
    out_ref[...] = mm(keys_ref[...], chain(later(me, sorted_slots(me, ins))))


def split3(x):
    hi = x.astype(BF16)
    rest = x - hi.astype(F32)
    mid = rest.astype(BF16)
    return hi, mid, (rest - mid.astype(F32)).astype(BF16)


def attend_kernel(stride, radix, heads, *refs):
    *ins, keys_ref, queries_ref, values_ref, out_ref = refs
    me = digit("seq", stride, radix)
    mats = later(me, sorted_slots(me, ins))
    width = keys_ref.shape[1]
    keys = mm(keys_ref[...], mats[0])
    rest = chain(mats[1:]) if len(mats) > 1 else None
    count = queries_ref.shape[0]
    dests, each = out_ref.shape[0], out_ref.shape[1]
    scale = 1.0 / (float(width) ** 0.5)
    lane = lax.broadcasted_iota(jnp.int32, (count, width), 1)
    stats = jnp.zeros((count, width), F32)
    for h in range(heads):
        q = queries_ref[:, h * width : (h + 1) * width].astype(F32)
        if rest is not None:
            q = mm_nt(q, rest)
        scores = mm_nt(q, keys) * scale
        peak = jnp.max(scores, axis=1, keepdims=True)
        expo = jnp.exp(scores - peak)
        total = jnp.sum(expo, axis=1, keepdims=True)
        numer = mm_fast(expo.astype(BF16), values_ref[...]) / total
        out_ref[:, :, h * width : (h + 1) * width] = numer.astype(BF16).reshape(dests, each, width)
        for i, part in enumerate(split3(peak) + split3(total)):
            stats = jnp.where(lane == h * 6 + i, part.astype(F32), stats)
    out_ref[:, :, heads * width :] = stats.astype(BF16).reshape(dests, each, width)


def merge(heads, width, got):
    stats = got[:, :, heads * width :].astype(F32)
    outs = []
    for h in range(heads):
        parts = [stats[:, :, h * 6 + i : h * 6 + i + 1] for i in range(6)]
        peak = parts[0] + parts[1] + parts[2]
        total = parts[3] + parts[4] + parts[5]
        weight = total * jnp.exp(peak - jnp.max(peak, axis=0, keepdims=True))
        weight = weight / jnp.sum(weight, axis=0, keepdims=True)
        numer = got[:, :, h * width : (h + 1) * width].astype(F32)
        outs.append(jnp.sum(weight * numer, axis=0))
    return outs


def merge_kernel(heads, halves, got_ref, out_ref):
    width = got_ref.shape[2] // (heads + 1)
    merged = merge(heads, width, got_ref[...])
    dests = out_ref.shape[0] // halves
    part = merged[0].shape[0] // halves
    stacked = jnp.concatenate(merged, axis=0).astype(BF16)
    rows = stacked.shape[0]
    row, col = iotas(rows, rows)
    p, h, j = row // (heads * part), (row // part) % heads, row % part
    pick = jnp.where(col == h * (halves * part) + p * part + j, 1.0, 0.0).astype(BF16)
    placed = mm_fast(pick, stacked).astype(BF16)
    each = heads * part
    for p in range(halves):
        piece = placed[p * each : (p + 1) * each]
        for s in range(dests):
            out_ref[s * halves + p] = piece


def project_kernel(heads, halves, got_ref, *refs):
    *w_refs, out_ref = refs
    me = lax.axis_index("head")
    sources, each, width = got_ref.shape
    part = each // heads
    rows = sources * each
    got = got_ref[...].reshape(rows, width)
    count = (sources // halves) * part
    row, col = iotas(rows, rows)
    g, h, s, j = row // (heads * count), (row // count) % heads, (row % count) // part, row % part
    pick = jnp.where(col == ((s * halves + g) * heads + h) * part + j, 1.0, 0.0).astype(BF16)
    placed = mm_fast(pick, got).astype(BF16)
    acc = jnp.zeros(out_ref.shape, F32)
    for k in range(halves):
        for h in range(heads):
            w = w_refs[0][h * width : (h + 1) * width, :]
            o = w_refs[1][h * width : (h + 1) * width, :] if halves > 1 else w
            w = jnp.where(me == k, w, o)
            lo = (k * heads + h) * count
            acc = acc + mm_fast(placed[lo : lo + count], w)
    out_ref[...] = acc.astype(BF16)


def radices(size):
    found = []
    while size % 4 == 0:
        found.append(4)
        size //= 4
    while size % 2 == 0:
        found.append(2)
        size //= 2
    assert size == 1
    return found


def exchange(x, devices, stride, radix):
    got = [x]
    for k in range(1, radix):
        pairs = []
        for i in range(devices):
            d = (i // stride) % radix
            pairs.append((i, i + ((d ^ k) - d) * stride))
        got.append(lax.ppermute(x, "seq", pairs))
    return got


def on_device(shards, halves, queries, keys, values, householder, out_proj):
    ctx_rows, width = keys.shape
    count = queries.shape[0]
    heads = queries.shape[1] // width
    each = count // shards
    direct = halves == 2 and each % halves == 0
    parts = (halves, each // halves) if direct else (1, each)
    square = jax.ShapeDtypeStruct((width, width), F32)
    tall = jax.ShapeDtypeStruct((ctx_rows, width), F32)
    blocks = ctx_rows // BLOCK
    if direct:
        other_w = lax.ppermute(out_proj, "head", [(0, 1), (1, 0)])
    total, unit, u, mats = call(
        spans_kernel,
        [square, tall, tall, jax.ShapeDtypeStruct((blocks, width, width), F32)],
        1 << 30,
    )(householder)
    rounds = []
    stride = 1
    for radix in radices(shards):
        rounds.append((stride, radix))
        stride *= radix
    carried = mixed_q = None
    for i, (stride, radix) in enumerate(rounds):
        got = exchange(total, shards, stride, radix)
        if i == 0:
            carried, mixed_q = call(
                functools.partial(carry_kernel, parts),
                [tall, jax.ShapeDtypeStruct(queries.shape, BF16)],
                1 << 31,
            )(keys, unit, u, mats, queries)
        if i + 1 < len(rounds):
            total = call(functools.partial(total_kernel, stride, radix), square, 1 << 28)(*got)
            carried = call(functools.partial(shift_kernel, stride, radix), tall, 1 << 30)(
                *got, carried
            )
    packed = call(
        functools.partial(attend_kernel, stride, radix, heads),
        jax.ShapeDtypeStruct((shards, each, (heads + 1) * width), BF16),
        1 << 31,
    )(*got, carried, mixed_q, values)
    packed = lax.all_to_all(packed, "seq", split_axis=0, concat_axis=0, tiled=True)
    if direct:
        spread = call(
            functools.partial(merge_kernel, heads, halves),
            jax.ShapeDtypeStruct((shards * halves, heads * each // halves, width), BF16),
            1 << 26,
        )(packed)
        spread = lax.all_to_all(spread, ("seq", "head"), split_axis=0, concat_axis=0, tiled=True)
        return call(
            functools.partial(project_kernel, heads, halves),
            jax.ShapeDtypeStruct((count // halves, out_proj.shape[1]), BF16),
            1 << 28,
        )(spread, out_proj, other_w)
    rows = jnp.concatenate(merge(heads, width, packed), axis=1).astype(BF16)
    attention = lax.all_gather(rows, "seq", axis=0, tiled=True)
    mixed = jnp.dot(attention, out_proj, preferred_element_type=F32).astype(BF16)
    return lax.psum_scatter(mixed, "head", scatter_dimension=0, tiled=True)


def solution(mesh):
    placed = (
        P(None, "head"),
        P("seq", "head"),
        P("seq", "head"),
        P("seq", "head"),
        P("head", "seq"),
    )
    body = functools.partial(on_device, mesh.shape["seq"], mesh.shape["head"])
    return jax.shard_map(
        body, mesh=mesh, in_specs=placed, out_specs=P("head", "seq"), check_vma=False
    )
```

time: 199 us -> 64.9 us (0.33)
  waiting for transfers between devices: 76.9 us -> 13.3 us
  blocking collectives: 48.2 us -> 12.1 us
  Pallas kernels: 0 us -> 25.2 us
  other arithmetic: 22 us -> 0 us
  local copies, waits for them, and re-layouts: 16.7 us -> 2.03 us
  between operations: 13.9 us -> 0.07 us
  matrix products: 12.9 us -> 0 us
  starting transfers between devices: 8.03 us -> 11.8 us
    all_gather x1 -> x0, waiting for transfers between devices: 57.9 us -> none  [on_device(): all_trans = lax.all_gather(shard_mat[None], 'seq', axis=0, tiled=True)]
    all_gather x1 -> x0, blocking collectives: 38.1 us -> none  [on_device(): attention = lax.all_gather(own_rows, 'seq', axis=1, tiled=True)]
    pallas_call x0 -> x7, Pallas kernels: none -> 25.2 us  [the longest x1 7.81 us: on_device(): call(spans_kernel, [square, tall, tall, jax.ShapeDtypeStruct((blocks, wid...]
    another operation x3 -> x0, other arithmetic: 19.7 us -> none  [the longest x1 19.7 us: span_forms(): coeff = jax.scipy.linalg.solve_triangular(lower, identity_block, lower=True)]
    dot_general x31 -> x0, matrix products: 12.5 us -> none  [the longest x7 2.61 us: compose_batch(): jnp.einsum('nab,nbc->nac', earlier, later, precision=lax.Precision.HIGHEST)]
    dynamic_update_slice x12 -> x0, local copies, waits for them, and re-layouts: 12 us -> none  [on_device(): peaks, totals, numerators = lax.map(attend, turned)]
    ppermute x0 -> x7, starting transfers between devices: none -> 9.06 us  [the longest x6 8.88 us: exchange(): got.append(lax.ppermute(x, 'seq', pairs))]
    all_to_all x2 -> x1, waiting for transfers between devices: 15.4 us -> 6.64 us  [on_device(): lax.all_to_all(spread, ('seq', 'head'), split_axis=0, concat_axis=0, tile...]
  transfers between devices with their start and end apart: 4 -> 8, of which waited for: 4 -> 5; matrix products, arithmetic and copies ran while one was open for 0% -> 0% of each run, Pallas kernels for 0% -> 9%
where the time goes in v1:
time: 64.9 us; the launch traced here: 64.4 us
  Pallas kernels  25.2 us (39%)
  waiting for transfers between devices  13.3 us (20%)
  blocking collectives  12.1 us (19%)
  starting transfers between devices  11.8 us (18%)
  local copies, waits for them, and re-layouts  2.03 us (3%)
    all_to_all x1, blocking collectives, on_device(): lax.all_to_all(packed, 'seq', split_axis=0, concat_axis=0, tiled=True)  12.1 us
    ppermute x6, starting transfers between devices, exchange(): got.append(lax.ppermute(x, 'seq', pairs))  8.88 us
    pallas_call x1, Pallas kernels, on_device(): call(spans_kernel, [square, tall, tall, jax.ShapeDtypeStruct((blocks, wid...  7.81 us
    all_to_all x1, waiting for transfers between devices, on_device(): lax.all_to_all(spread, ('seq', 'head'), split_axis=0, concat_axis=0, tile...  6.64 us
    ppermute x6, waiting for transfers between devices, exchange(): got.append(lax.ppermute(x, 'seq', pairs))  5.4 us
    pallas_call x1, Pallas kernels, on_device(): call(functools.partial(attend_kernel, stride, radix, heads), jax.ShapeDty...  5.04 us
    pallas_call x1, Pallas kernels, on_device(): call(functools.partial(carry_kernel, parts), [tall, jax.ShapeDtypeStruct(...  3.6 us
    all_to_all x1, starting transfers between devices, on_device(): lax.all_to_all(spread, ('seq', 'head'), split_axis=0, concat_axis=0, tile...  2.7 us
  transfers between devices with their start and end apart: 8, of which 5 were waited for; matrix products, arithmetic and copies ran while one was open for 0% of the time, Pallas kernels for 9%

profile of v1, /device:TPU:0, one launch (start us, length us, event | category | flops | bytes accessed | tf_op | source)
XLA Modules:
  0.0 64.4 jit_solution(6212518892001504921)
XLA Ops:
  0.0 7.8 %shard_map.55 = (f32[128,128]{1,0:T(8,128)}, f32[256,128]{1,0:T(8,128)}, f32[256,128]{1,0:T(8,128)}, f32[4,128,128]{2,1,0:T(8,128)}) custom-call(bf16[256,128]{1,0:T(8,128)(2,1)} %raw_ref.1), custom_call_target="tpu_custom_call" | custom-call | flops 1073741824 | bytes 1048576 | tf_op jit(solution)/shard_map/pallas_call | solution.py:281
  7.8 3.0 %collective-permute-start = (f32[128,128]{1,0:T(8,128)}, f32[128,128]{1,0:T(8,128)S(1)}, u32[]{:S(2)}, u32[]{:S(2)}) collective-permute-start(f32[128,128]{1,0:T(8,128)} %get-tuple-element.11.refs_0_), channel_id=1, source_target_pairs={{0,2},{2,0},{4,6},{6,4},{8,10},{10,8},{12,14},{14,12},{16,18},{18,... | collective-permute-start | bytes 196616 | tf_op jit(solution)/shard_map/ppermute | solution.py:265
  10.8 1.5 %collective-permute-start.1 = (f32[128,128]{1,0:T(8,128)}, f32[128,128]{1,0:T(8,128)S(1)}, u32[]{:S(2)}, u32[]{:S(2)}) collective-permute-start(f32[128,128]{1,0:T(8,128)} %get-tuple-element.11.refs_0_), channel_id=1, source_target_pairs={{0,4},{2,6},{4,0},{6,2},{8,12},{10,14},{12,8},{14,10},{16,20},{18,... | collective-permute-start | bytes 196616 | tf_op jit(solution)/shard_map/ppermute | solution.py:265
  12.3 0.0 collective-permute-start.2
  12.3 3.6 %shard_map.57 = (f32[256,128]{1,0:T(8,128)}, bf16[128,512]{1,0:T(8,128)(2,1)}) custom-call(bf16[256,128]{1,0:T(8,128)(2,1)} %keys_ref.1, f32[256,128]{1,0:T(8,128)} %get-tuple-element.12.unit_ref, f32[256,128]{1,0:T(8,128)} %get-tuple-element.13.u_ref, f32[4,128,128]{2,1,0:T(8,128)} %get-tuple-element.14.parts_ref, bf16[128,512]{1,0:T(8,128)(2,1)} %queries_ref.1), custom_call_target="tpu_custom_call" | custom-call | flops 2147483648 | bytes 1048576 | tf_op jit(solution)/shard_map/pallas_call | solution.py:295
  15.9 0.0 collective-permute-done.refs_1_
  15.9 0.0 copy-start.4
  15.9 0.0 collective-permute-done.1.refs_2_
  15.9 0.0 copy-start.5
  15.9 1.7 %collective-permute-done.2.refs_3_ = f32[128,128]{1,0:T(8,128)S(1)} collective-permute-done((f32[128,128]{1,0:T(8,128)}, f32[128,128]{1,0:T(8,128)S(1)}, u32[]{:S(2)}, u32[]{:S(2)}) %collective-permute-start.2) | collective-permute-done | bytes 65568 | tf_op jit(solution)/shard_map/ppermute | solution.py:265
  17.7 0.0 copy-done.4
  17.7 0.0 copy-done.5
  17.7 0.0 copy-start.6
  17.7 0.6 copy-done.6
  18.3 2.1 %shard_map.56.refs_0_ = f32[128,128]{1,0:T(8,128)} custom-call(f32[128,128]{1,0:T(8,128)} %get-tuple-element.11.refs_0_, f32[128,128]{1,0:T(8,128)} %copy-done.4, f32[128,128]{1,0:T(8,128)} %copy-done.5, f32[128,128]{1,0:T(8,128)} %copy-done.6), custom_call_target="tpu_custom_call" | custom-call | flops 268435456 | bytes 1048576 | tf_op jit(solution)/shard_map/pallas_call | solution.py:301
  20.4 1.6 %collective-permute-start.3 = (f32[128,128]{1,0:T(8,128)}, f32[128,128]{1,0:T(8,128)S(1)}, u32[]{:S(2)}, u32[]{:S(2)}) collective-permute-start(f32[128,128]{1,0:T(8,128)} %shard_map.56.refs_0_), channel_id=1, source_target_pairs={{0,8},{2,10},{4,12},{6,14},{8,0},{10,2},{12,4},{14,6},{16,24},{18,... | collective-permute-start | bytes 196616 | tf_op jit(solution)/shard_map/ppermute | solution.py:265
  22.0 2.6 %collective-permute-start.4 = (f32[128,128]{1,0:T(8,128)}, f32[128,128]{1,0:T(8,128)S(1)}, u32[]{:S(2)}, u32[]{:S(2)}) collective-permute-start(f32[128,128]{1,0:T(8,128)} %shard_map.56.refs_0_), channel_id=1, source_target_pairs={{0,16},{2,18},{4,20},{6,22},{8,24},{10,26},{12,28},{14,30},{16,0},... | collective-permute-start | bytes 196616 | tf_op jit(solution)/shard_map/ppermute | solution.py:265
  24.6 0.2 collective-permute-start.5
  24.8 2.4 %shard_map.58.refs_4_ = f32[256,128]{1,0:T(8,128)} custom-call(f32[128,128]{1,0:T(8,128)} %get-tuple-element.11.refs_0_, f32[128,128]{1,0:T(8,128)} %copy-done.4, f32[128,128]{1,0:T(8,128)} %copy-done.5, f32[128,128]{1,0:T(8,128)} %copy-done.6, f32[256,128]{1,0:T(8,128)} %get-tuple-element.15.refs_4_), custom_call_target="tpu_custom_call" | custom-call | flops 1073741824 | bytes 1048576 | tf_op jit(solution)/shard_map/pallas_call | solution.py:302
  27.2 0.0 collective-permute-done.3.refs_1_
  27.2 0.0 copy-start.7
  27.2 1.6 %collective-permute-done.4.refs_2_ = f32[128,128]{1,0:T(8,128)S(1)} collective-permute-done((f32[128,128]{1,0:T(8,128)}, f32[128,128]{1,0:T(8,128)S(1)}, u32[]{:S(2)}, u32[]{:S(2)}) %collective-permute-start.4) | collective-permute-done | bytes 65568 | tf_op jit(solution)/shard_map/ppermute | solution.py:265
  28.8 0.0 copy-start.8
  28.8 2.1 %collective-permute-done.5.refs_3_ = f32[128,128]{1,0:T(8,128)S(1)} collective-permute-done((f32[128,128]{1,0:T(8,128)}, f32[128,128]{1,0:T(8,128)S(1)}, u32[]{:S(2)}, u32[]{:S(2)}) %collective-permute-start.5) | collective-permute-done | bytes 65568 | tf_op jit(solution)/shard_map/ppermute | solution.py:265
  30.8 0.0 copy-start.9
  30.8 0.0 copy-done.7
  30.8 0.0 copy-done.8
  30.8 0.6 copy-done.9
  31.5 5.0 %shard_map.59 = bf16[16,8,640]{2,1,0:T(8,128)(2,1)} custom-call(f32[128,128]{1,0:T(8,128)} %shard_map.56.refs_0_, f32[128,128]{1,0:T(8,128)} %copy-done.7, f32[128,128]{1,0:T(8,128)} %copy-done.8, f32[128,128]{1,0:T(8,128)} %copy-done.9, f32[256,128]{1,0:T(8,128)} %shard_map.58.refs_4_, bf16[128,512]{1,0:T(8,128)(2,1)} %get-tuple-element.16.refs_5_, ...), custom_call_target="tpu_custom_call" | custom-call | flops 2147483648 | bytes 1048576 | tf_op jit(solution)/shard_map/pallas_call | solution.py:305
  36.5 12.1 %all_to_all.10.got_ref = bf16[16,8,640]{2,1,0:T(8,128)(2,1)} all-to-all(bf16[16,8,640]{2,1,0:T(8,128)(2,1)} %shard_map.59), channel_id=1, replica_groups=mesh['seq'=16,'head'=2] {'seq'}, dimensions={0} | all-to-all | bytes 327680 | tf_op jit(solution)/shard_map/all_to_all | solution.py:310
  48.6 2.1 %shard_map.60 = bf16[32,16,128]{2,1,0:T(8,128)(2,1)} custom-call(bf16[16,8,640]{2,1,0:T(8,128)(2,1)} %all_to_all.10.got_ref), custom_call_target="tpu_custom_call" | custom-call | flops 67108864 | bytes 1048576 | tf_op jit(solution)/shard_map/pallas_call | solution.py:312
  50.7 0.0 copy-start.2
  50.7 2.7 %all-to-all-start.1 = ((bf16[32,16,128]{2,1,0:T(8,128)(2,1)}), bf16[32,16,128]{2,1,0:T(8,128)(2,1)S(1)}, u32[]{:S(2)}, u32[]{:S(2)}) async-start(bf16[32,16,128]{2,1,0:T(8,128)(2,1)} %shard_map.60), calls=%async_computation.1 | async-start | bytes 262144 | tf_op jit(solution)/shard_map/all_to_all | solution.py:317
  53.4 0.0 copy-done.2
  53.4 0.1 copy.7.refs_0_
  53.6 0.0 copy-start
  53.6 0.2 collective-permute-start.6
  53.8 1.2 %collective-permute-done.6.refs_1_ = bf16[512,64]{1,0:T(8,128)(2,1)S(1)} collective-permute-done((bf16[512,64]{1,0:T(8,128)(2,1)S(1)}, bf16[512,64]{1,0:T(8,128)(2,1)S(1)}, u32[]{:S(2)}, u32[]{:S(2)}) %collective-permute-start.6) | collective-permute-done | bytes 65568 | tf_op jit(solution)/shard_map/ppermute | solution.py:280
  55.0 0.0 copy-start.3
  55.0 6.6 %all-to-all-done.1.got_ref = bf16[32,16,128]{2,1,0:T(8,128)(2,1)S(1)} async-done(((bf16[32,16,128]{2,1,0:T(8,128)(2,1)}), bf16[32,16,128]{2,1,0:T(8,128)(2,1)S(1)}, u32[]{:S(2)}, u32[]{:S(2)}) %all-to-all-start.1) | async-done | bytes 131104 | tf_op jit(solution)/shard_map/all_to_all | solution.py:317
  61.6 0.0 copy-done
  61.6 0.0 copy-done.3
  61.6 0.0 copy-start.1
  61.6 0.6 %copy-done.1 = bf16[32,16,128]{2,1,0:T(8,128)(2,1)} copy-done((bf16[32,16,128]{2,1,0:T(8,128)(2,1)}, bf16[32,16,128]{2,1,0:T(8,128)(2,1)S(1)}, u32[]{:S(2)}) %copy-start.1) | copy-done | bytes 131096
  62.3 2.2 %shard_map.61 = bf16[64,64]{1,0:T(8,128)(2,1)} custom-call(bf16[32,16,128]{2,1,0:T(8,128)(2,1)} %copy-done.1, bf16[512,64]{1,0:T(8,128)(2,1)} %copy-done, bf16[512,64]{1,0:T(8,128)(2,1)} %copy-done.3), custom_call_target="tpu_custom_call" | custom-call | flops 268435456 | bytes 1048576 | tf_op jit(solution)/shard_map/pallas_call | solution.py:318
Async XLA Ops:
  7.8 8.1 %collective-permute-start = (f32[128,128]{1,0:T(8,128)}, f32[128,128]{1,0:T(8,128)S(1)}, u32[]{:S(2)}, u32[]{:S(2)}) collective-permute-start(f32[128,128]{1,0:T(8,128)} %get-tuple-element.11.refs_0_), channel_id=1, source_target_pairs={{0,2},{2,0},{4,6},{6,4},{8,10},{10,8},{12,14},{14,12},{16,18},{18,... | collective-permute-start | bytes 196616 | tf_op jit(solution)/shard_map/ppermute | solution.py:265
  10.8 5.1 %collective-permute-start.1 = (f32[128,128]{1,0:T(8,128)}, f32[128,128]{1,0:T(8,128)S(1)}, u32[]{:S(2)}, u32[]{:S(2)}) collective-permute-start(f32[128,128]{1,0:T(8,128)} %get-tuple-element.11.refs_0_), channel_id=1, source_target_pairs={{0,4},{2,6},{4,0},{6,2},{8,12},{10,14},{12,8},{14,10},{16,20},{18,... | collective-permute-start | bytes 196616 | tf_op jit(solution)/shard_map/ppermute | solution.py:265
  12.3 5.4 %collective-permute-start.2 = (f32[128,128]{1,0:T(8,128)}, f32[128,128]{1,0:T(8,128)S(1)}, u32[]{:S(2)}, u32[]{:S(2)}) collective-permute-start(f32[128,128]{1,0:T(8,128)} %get-tuple-element.11.refs_0_), channel_id=1, source_target_pairs={{0,6},{2,4},{4,2},{6,0},{8,14},{10,12},{12,10},{14,8},{16,22},{18,... | collective-permute-start | bytes 196616 | tf_op jit(solution)/shard_map/ppermute | solution.py:265
  15.9 1.8 %copy-start.4 = (f32[128,128]{1,0:T(8,128)}, f32[128,128]{1,0:T(8,128)S(1)}, u32[]{:S(2)}) copy-start(f32[128,128]{1,0:T(8,128)S(1)} %collective-permute-done.refs_1_) | copy-start | bytes 196612
  15.9 1.8 %copy-start.5 = (f32[128,128]{1,0:T(8,128)}, f32[128,128]{1,0:T(8,128)S(1)}, u32[]{:S(2)}) copy-start(f32[128,128]{1,0:T(8,128)S(1)} %collective-permute-done.1.refs_2_) | copy-start | bytes 196612
  17.7 0.6 copy-start.6
  20.4 6.8 %collective-permute-start.3 = (f32[128,128]{1,0:T(8,128)}, f32[128,128]{1,0:T(8,128)S(1)}, u32[]{:S(2)}, u32[]{:S(2)}) collective-permute-start(f32[128,128]{1,0:T(8,128)} %shard_map.56.refs_0_), channel_id=1, source_target_pairs={{0,8},{2,10},{4,12},{6,14},{8,0},{10,2},{12,4},{14,6},{16,24},{18,... | collective-permute-start | bytes 196616 | tf_op jit(solution)/shard_map/ppermute | solution.py:265
  22.0 6.8 %collective-permute-start.4 = (f32[128,128]{1,0:T(8,128)}, f32[128,128]{1,0:T(8,128)S(1)}, u32[]{:S(2)}, u32[]{:S(2)}) collective-permute-start(f32[128,128]{1,0:T(8,128)} %shard_map.56.refs_0_), channel_id=1, source_target_pairs={{0,16},{2,18},{4,20},{6,22},{8,24},{10,26},{12,28},{14,30},{16,0},... | collective-permute-start | bytes 196616 | tf_op jit(solution)/shard_map/ppermute | solution.py:265
  24.6 6.3 %collective-permute-start.5 = (f32[128,128]{1,0:T(8,128)}, f32[128,128]{1,0:T(8,128)S(1)}, u32[]{:S(2)}, u32[]{:S(2)}) collective-permute-start(f32[128,128]{1,0:T(8,128)} %shard_map.56.refs_0_), channel_id=1, source_target_pairs={{0,24},{2,26},{4,28},{6,30},{8,16},{10,18},{12,20},{14,22},{16,8},... | collective-permute-start | bytes 196616 | tf_op jit(solution)/shard_map/ppermute | solution.py:265
  27.2 3.7 %copy-start.7 = (f32[128,128]{1,0:T(8,128)}, f32[128,128]{1,0:T(8,128)S(1)}, u32[]{:S(2)}) copy-start(f32[128,128]{1,0:T(8,128)S(1)} %collective-permute-done.3.refs_1_) | copy-start | bytes 196612
  28.8 2.1 %copy-start.8 = (f32[128,128]{1,0:T(8,128)}, f32[128,128]{1,0:T(8,128)S(1)}, u32[]{:S(2)}) copy-start(f32[128,128]{1,0:T(8,128)S(1)} %collective-permute-done.4.refs_2_) | copy-start | bytes 196612
  30.8 0.6 copy-start.9
  50.7 2.7 %copy-start.2 = (bf16[512,64]{0,1:T(8,128)(2,1)S(1)}, bf16[512,64]{0,1:T(8,128)(2,1)}, u32[]{:S(2)}) copy-start(bf16[512,64]{0,1:T(8,128)(2,1)} %param.9) | copy-start | bytes 196612
  50.7 10.9 %all-to-all-start.1 = ((bf16[32,16,128]{2,1,0:T(8,128)(2,1)}), bf16[32,16,128]{2,1,0:T(8,128)(2,1)S(1)}, u32[]{:S(2)}, u32[]{:S(2)}) async-start(bf16[32,16,128]{2,1,0:T(8,128)(2,1)} %shard_map.60), calls=%async_computation.1 | async-start | bytes 262144 | tf_op jit(solution)/shard_map/all_to_all | solution.py:317
  53.6 8.1 %copy-start = (bf16[512,64]{1,0:T(8,128)(2,1)}, bf16[512,64]{1,0:T(8,128)(2,1)S(1)}, u32[]{:S(2)}) copy-start(bf16[512,64]{1,0:T(8,128)(2,1)S(1)} %copy.7.refs_0_) | copy-start | bytes 196612
  53.6 1.4 %collective-permute-start.6 = (bf16[512,64]{1,0:T(8,128)(2,1)S(1)}, bf16[512,64]{1,0:T(8,128)(2,1)S(1)}, u32[]{:S(2)}, u32[]{:S(2)}) collective-permute-start(bf16[512,64]{1,0:T(8,128)(2,1)S(1)} %copy.7.refs_0_), channel_id=1, source_target_pairs={{0,1},{1,0},{2,3},{3,2},{4,5},{5,4},{6,7},{7,6},{8,9},{9,8},{10,11... | collective-permute-start | bytes 196616 | tf_op jit(solution)/shard_map/ppermute | solution.py:280
  55.0 6.7 %copy-start.3 = (bf16[512,64]{1,0:T(8,128)(2,1)}, bf16[512,64]{1,0:T(8,128)(2,1)S(1)}, u32[]{:S(2)}) copy-start(bf16[512,64]{1,0:T(8,128)(2,1)S(1)} %collective-permute-done.6.refs_1_) | copy-start | bytes 196612
  61.6 0.6 %copy-start.1 = (bf16[32,16,128]{2,1,0:T(8,128)(2,1)}, bf16[32,16,128]{2,1,0:T(8,128)(2,1)S(1)}, u32[]{:S(2)}) copy-start(bf16[32,16,128]{2,1,0:T(8,128)(2,1)S(1)} %all-to-all-done.1.got_ref) | copy-start | bytes 393220

commit v2 on v1

--- a/solution.py
+++ b/solution.py
@@ -8,6 +8,7 @@
 from jax.sharding import PartitionSpec as P
 
 BLOCK = 64
+LIMIT = 16 << 20
 F32 = jnp.float32
 BF16 = jnp.bfloat16
 VMEM = pl.BlockSpec(memory_space=pltpu.VMEM)
@@ -59,6 +60,7 @@
         kernel,
         out_shape=outs if single else list(many),
         cost_estimate=pl.CostEstimate(flops=flops, bytes_accessed=1 << 20, transcendentals=0),
+        compiler_params=pltpu.CompilerParams(vmem_limit_bytes=LIMIT),
         **kw,
     )
 

time: 64.9 us -> 55.1 us (0.85)
  Pallas kernels: 25.2 us -> 15 us
  waiting for transfers between devices: 13.3 us -> 16.3 us
  blocking collectives: 12.1 us -> 10.5 us
  local copies, waits for them, and re-layouts: 2.03 us -> 1.01 us
    ppermute x6, waiting for transfers between devices: 5.4 us -> 8.46 us  [exchange(): got.append(lax.ppermute(x, 'seq', pairs))]
    pallas_call x1, Pallas kernels: 3.6 us -> 1.8 us  [on_device(): call(functools.partial(carry_kernel, parts), [tall, jax.ShapeDtypeStruct(...]
    pallas_call x1, Pallas kernels: 5.04 us -> 3.27 us  [on_device(): call(functools.partial(attend_kernel, stride, radix, heads), jax.ShapeDty...]
    pallas_call x1, Pallas kernels: 2.4 us -> 0.71 us  [on_device(): call(functools.partial(shift_kernel, stride, radix), tall, 1 << 30)]
    all_to_all x1, blocking collectives: 12.1 us -> 10.5 us  [on_device(): lax.all_to_all(packed, 'seq', split_axis=0, concat_axis=0, tiled=True)]
    pallas_call x1, Pallas kernels: 2.1 us -> 0.54 us  [on_device(): call(functools.partial(total_kernel, stride, radix), square, 1 << 28)(*got)]
    pallas_call x1, Pallas kernels: 7.81 us -> 6.33 us  [on_device(): call(spans_kernel, [square, tall, tall, jax.ShapeDtypeStruct((blocks, wid...]
    unnamed x21 -> x11, local copies, waits for them, and re-layouts: 2.03 us -> 1.01 us
  transfers between devices with their start and end apart: 8 -> 8, of which waited for: 5 -> 6; matrix products, arithmetic and copies ran while one was open for 0% -> 0% of each run, Pallas kernels for 9% -> 5%
where the time goes in v2:
time: 55.1 us; the launch traced here: 54.8 us
  waiting for transfers between devices  16.3 us (30%)
  Pallas kernels  15 us (27%)
  starting transfers between devices  11.9 us (22%)
  blocking collectives  10.5 us (19%)
  local copies, waits for them, and re-layouts  1.01 us (2%)
    all_to_all x1, blocking collectives, on_device(): lax.all_to_all(packed, 'seq', split_axis=0, concat_axis=0, tiled=True)  10.5 us
    ppermute x6, starting transfers between devices, exchange(): got.append(lax.ppermute(x, 'seq', pairs))  9.03 us
    ppermute x6, waiting for transfers between devices, exchange(): got.append(lax.ppermute(x, 'seq', pairs))  8.46 us
    all_to_all x1, waiting for transfers between devices, on_device(): lax.all_to_all(spread, ('seq', 'head'), split_axis=0, concat_axis=0, tile...  6.66 us
    pallas_call x1, Pallas kernels, on_device(): call(spans_kernel, [square, tall, tall, jax.ShapeDtypeStruct((blocks, wid...  6.33 us
    pallas_call x1, Pallas kernels, on_device(): call(functools.partial(attend_kernel, stride, radix, heads), jax.ShapeDty...  3.27 us
    all_to_all x1, starting transfers between devices, on_device(): lax.all_to_all(spread, ('seq', 'head'), split_axis=0, concat_axis=0, tile...  2.69 us
    pallas_call x1, Pallas kernels, on_device(): call(functools.partial(carry_kernel, parts), [tall, jax.ShapeDtypeStruct(...  1.8 us
  transfers between devices with their start and end apart: 8, of which 6 were waited for; matrix products, arithmetic and copies ran while one was open for 0% of the time, Pallas kernels for 5%

profile of v2, /device:TPU:0, one launch (start us, length us, event | category | flops | bytes accessed | tf_op | source)
XLA Modules:
  0.0 54.8 jit_solution(7949389959598094964)
XLA Ops:
  0.0 0.0 copy-start
  0.0 0.0 copy-start.1
  0.0 0.9 %copy-done.1 = bf16[256,128]{1,0:T(8,128)(2,1)S(1)} copy-done((bf16[256,128]{1,0:T(8,128)(2,1)S(1)}, bf16[256,128]{1,0:T(8,128)(2,1)}, u32[]{:S(2)}) %copy-start.1) | copy-done | bytes 65560
  0.9 0.0 copy-start.2
  0.9 6.3 %shard_map.55 = (f32[128,128]{1,0:T(8,128)S(1)}, f32[256,128]{1,0:T(8,128)S(1)}, f32[256,128]{1,0:T(8,128)S(1)}, f32[4,128,128]{2,1,0:T(8,128)S(1)}) custom-call(bf16[256,128]{1,0:T(8,128)(2,1)S(1)} %copy-done.1), custom_call_target="tpu_custom_call" | custom-call | flops 1073741824 | bytes 1048576 | tf_op jit(solution)/shard_map/pallas_call | solution.py:283
  7.2 3.0 %collective-permute-start = (f32[128,128]{1,0:T(8,128)S(1)}, f32[128,128]{1,0:T(8,128)S(1)}, u32[]{:S(2)}, u32[]{:S(2)}) collective-permute-start(f32[128,128]{1,0:T(8,128)S(1)} %get-tuple-element.11.refs_0_), channel_id=1, source_target_pairs={{0,2},{2,0},{4,6},{6,4},{8,10},{10,8},{12,14},{14,12},{16,18},{18,... | collective-permute-start | bytes 196616 | tf_op jit(solution)/shard_map/ppermute | solution.py:267
  10.3 1.5 %collective-permute-start.1 = (f32[128,128]{1,0:T(8,128)S(1)}, f32[128,128]{1,0:T(8,128)S(1)}, u32[]{:S(2)}, u32[]{:S(2)}) collective-permute-start(f32[128,128]{1,0:T(8,128)S(1)} %get-tuple-element.11.refs_0_), channel_id=1, source_target_pairs={{0,4},{2,6},{4,0},{6,2},{8,12},{10,14},{12,8},{14,10},{16,20},{18,... | collective-permute-start | bytes 196616 | tf_op jit(solution)/shard_map/ppermute | solution.py:267
  11.8 0.0 collective-permute-start.2
  11.8 0.0 copy-done
  11.8 0.0 copy-done.2
  11.8 1.8 %shard_map.57 = (f32[256,128]{1,0:T(8,128)S(1)}, bf16[128,512]{1,0:T(8,128)(2,1)S(1)}) custom-call(bf16[256,128]{1,0:T(8,128)(2,1)S(1)} %copy-done.2, f32[256,128]{1,0:T(8,128)S(1)} %get-tuple-element.12.unit_ref, f32[256,128]{1,0:T(8,128)S(1)} %get-tuple-element.13.u_ref, f32[4,128,128]{2,1,0:T(8,128)S(1)} %get-tuple-element.14.parts_ref, ...), custom_call_target="tpu_custom_call" | custom-call | flops 2147483648 | bytes 1048576 | tf_op jit(solution)/shard_map/pallas_call | solution.py:297
  13.6 0.0 collective-permute-done.refs_1_
  13.6 0.9 %collective-permute-done.1.refs_2_ = f32[128,128]{1,0:T(8,128)S(1)} collective-permute-done((f32[128,128]{1,0:T(8,128)S(1)}, f32[128,128]{1,0:T(8,128)S(1)}, u32[]{:S(2)}, u32[]{:S(2)}) %collective-permute-start.1) | collective-permute-done | bytes 65568 | tf_op jit(solution)/shard_map/ppermute | solution.py:267
  14.5 2.4 %collective-permute-done.2.refs_3_ = f32[128,128]{1,0:T(8,128)S(1)} collective-permute-done((f32[128,128]{1,0:T(8,128)S(1)}, f32[128,128]{1,0:T(8,128)S(1)}, u32[]{:S(2)}, u32[]{:S(2)}) %collective-permute-start.2) | collective-permute-done | bytes 65568 | tf_op jit(solution)/shard_map/ppermute | solution.py:267
  16.9 0.5 shard_map.56.refs_0_
  17.5 1.6 %collective-permute-start.3 = (f32[128,128]{1,0:T(8,128)S(1)}, f32[128,128]{1,0:T(8,128)S(1)}, u32[]{:S(2)}, u32[]{:S(2)}) collective-permute-start(f32[128,128]{1,0:T(8,128)S(1)} %shard_map.56.refs_0_), channel_id=1, source_target_pairs={{0,8},{2,10},{4,12},{6,14},{8,0},{10,2},{12,4},{14,6},{16,24},{18,... | collective-permute-start | bytes 196616 | tf_op jit(solution)/shard_map/ppermute | solution.py:267
  19.1 2.6 %collective-permute-start.4 = (f32[128,128]{1,0:T(8,128)S(1)}, f32[128,128]{1,0:T(8,128)S(1)}, u32[]{:S(2)}, u32[]{:S(2)}) collective-permute-start(f32[128,128]{1,0:T(8,128)S(1)} %shard_map.56.refs_0_), channel_id=1, source_target_pairs={{0,16},{2,18},{4,20},{6,22},{8,24},{10,26},{12,28},{14,30},{16,0},... | collective-permute-start | bytes 196616 | tf_op jit(solution)/shard_map/ppermute | solution.py:267
  21.7 0.2 collective-permute-start.5
  21.9 0.0 copy-start.3
  21.9 0.7 %shard_map.58.refs_4_ = f32[256,128]{1,0:T(8,128)S(1)} custom-call(f32[128,128]{1,0:T(8,128)S(1)} %get-tuple-element.11.refs_0_, f32[128,128]{1,0:T(8,128)S(1)} %collective-permute-done.refs_1_, f32[128,128]{1,0:T(8,128)S(1)} %collective-permute-done.1.refs_2_, f32[128,128]{1,0:T(8,128)S(1)} %collective-permute-done.2.refs_3_, ...), custom_call_target="tpu_custom_call" | custom-call | flops 1073741824 | bytes 1048576 | tf_op jit(solution)/shard_map/pallas_call | solution.py:304
  22.7 0.0 collective-permute-done.3.refs_1_
  22.7 3.0 %collective-permute-done.4.refs_2_ = f32[128,128]{1,0:T(8,128)S(1)} collective-permute-done((f32[128,128]{1,0:T(8,128)S(1)}, f32[128,128]{1,0:T(8,128)S(1)}, u32[]{:S(2)}, u32[]{:S(2)}) %collective-permute-start.4) | collective-permute-done | bytes 65568 | tf_op jit(solution)/shard_map/ppermute | solution.py:267
  25.7 2.1 %collective-permute-done.5.refs_3_ = f32[128,128]{1,0:T(8,128)S(1)} collective-permute-done((f32[128,128]{1,0:T(8,128)S(1)}, f32[128,128]{1,0:T(8,128)S(1)}, u32[]{:S(2)}, u32[]{:S(2)}) %collective-permute-start.5) | collective-permute-done | bytes 65568 | tf_op jit(solution)/shard_map/ppermute | solution.py:267
  27.8 0.0 copy-done.3
  27.8 3.3 %shard_map.59 = bf16[16,8,640]{2,1,0:T(8,128)(2,1)S(1)} custom-call(f32[128,128]{1,0:T(8,128)S(1)} %shard_map.56.refs_0_, f32[128,128]{1,0:T(8,128)S(1)} %collective-permute-done.3.refs_1_, f32[128,128]{1,0:T(8,128)S(1)} %collective-permute-done.4.refs_2_, f32[128,128]{1,0:T(8,128)S(1)} %collective-permute-done.5.refs_3_, f32[256,128]{1,0:T(8,128)S(1)} %shard_map.58.refs_4_, ...), custom_call_target="tpu_custom_call" | custom-call | flops 2147483648 | bytes 1048576 | tf_op jit(solution)/shard_map/pallas_call | solution.py:307
  31.1 10.5 %all_to_all.10.got_ref = bf16[16,8,640]{2,1,0:T(8,128)(2,1)S(1)} all-to-all(bf16[16,8,640]{2,1,0:T(8,128)(2,1)S(1)} %shard_map.59), channel_id=1, replica_groups=mesh['seq'=16,'head'=2] {'seq'}, dimensions={0} | all-to-all | bytes 327680 | tf_op jit(solution)/shard_map/all_to_all | solution.py:312
  41.6 1.2 %shard_map.60 = bf16[32,16,128]{2,1,0:T(8,128)(2,1)} custom-call(bf16[16,8,640]{2,1,0:T(8,128)(2,1)S(1)} %all_to_all.10.got_ref), custom_call_target="tpu_custom_call" | custom-call | flops 67108864 | bytes 1048576 | tf_op jit(solution)/shard_map/pallas_call | solution.py:314
  42.8 0.0 copy-start.4
  42.8 2.7 %all-to-all-start.1 = ((bf16[32,16,128]{2,1,0:T(8,128)(2,1)}), bf16[32,16,128]{2,1,0:T(8,128)(2,1)S(1)}, u32[]{:S(2)}, u32[]{:S(2)}) async-start(bf16[32,16,128]{2,1,0:T(8,128)(2,1)} %shard_map.60), calls=%async_computation.1 | async-start | bytes 262144 | tf_op jit(solution)/shard_map/all_to_all | solution.py:319
  45.5 0.0 copy-done.4
  45.5 0.1 copy.7.refs_0_
  45.6 0.2 collective-permute-start.6
  45.8 1.2 %collective-permute-done.6.refs_1_ = bf16[512,64]{1,0:T(8,128)(2,1)S(1)} collective-permute-done((bf16[512,64]{1,0:T(8,128)(2,1)S(1)}, bf16[512,64]{1,0:T(8,128)(2,1)S(1)}, u32[]{:S(2)}, u32[]{:S(2)}) %collective-permute-start.6) | collective-permute-done | bytes 65568 | tf_op jit(solution)/shard_map/ppermute | solution.py:282
  47.0 6.7 %all-to-all-done.1.got_ref = bf16[32,16,128]{2,1,0:T(8,128)(2,1)S(1)} async-done(((bf16[32,16,128]{2,1,0:T(8,128)(2,1)}), bf16[32,16,128]{2,1,0:T(8,128)(2,1)S(1)}, u32[]{:S(2)}, u32[]{:S(2)}) %all-to-all-start.1) | async-done | bytes 131104 | tf_op jit(solution)/shard_map/all_to_all | solution.py:319
  53.7 1.1 %shard_map.61 = bf16[64,64]{1,0:T(8,128)(2,1)} custom-call(bf16[32,16,128]{2,1,0:T(8,128)(2,1)S(1)} %all-to-all-done.1.got_ref, bf16[512,64]{1,0:T(8,128)(2,1)S(1)} %copy.7.refs_0_, bf16[512,64]{1,0:T(8,128)(2,1)S(1)} %collective-permute-done.6.refs_1_), custom_call_target="tpu_custom_call" | custom-call | flops 268435456 | bytes 1048576 | tf_op jit(solution)/shard_map/pallas_call | solution.py:320
Async XLA Ops:
  0.0 11.8 %copy-start = (bf16[128,512]{1,0:T(8,128)(2,1)S(1)}, bf16[128,512]{1,0:T(8,128)(2,1)}, u32[]{:S(2)}) copy-start(bf16[128,512]{1,0:T(8,128)(2,1)} %queries_ref.1) | copy-start | bytes 393220
  0.0 0.9 %copy-start.1 = (bf16[256,128]{1,0:T(8,128)(2,1)S(1)}, bf16[256,128]{1,0:T(8,128)(2,1)}, u32[]{:S(2)}) copy-start(bf16[256,128]{1,0:T(8,128)(2,1)} %raw_ref.1) | copy-start | bytes 196612
  0.9 10.9 %copy-start.2 = (bf16[256,128]{1,0:T(8,128)(2,1)S(1)}, bf16[256,128]{1,0:T(8,128)(2,1)}, u32[]{:S(2)}) copy-start(bf16[256,128]{1,0:T(8,128)(2,1)} %keys_ref.1) | copy-start | bytes 196612
  7.2 6.4 %collective-permute-start = (f32[128,128]{1,0:T(8,128)S(1)}, f32[128,128]{1,0:T(8,128)S(1)}, u32[]{:S(2)}, u32[]{:S(2)}) collective-permute-start(f32[128,128]{1,0:T(8,128)S(1)} %get-tuple-element.11.refs_0_), channel_id=1, source_target_pairs={{0,2},{2,0},{4,6},{6,4},{8,10},{10,8},{12,14},{14,12},{16,18},{18,... | collective-permute-start | bytes 196616 | tf_op jit(solution)/shard_map/ppermute | solution.py:267
  10.3 4.3 %collective-permute-start.1 = (f32[128,128]{1,0:T(8,128)S(1)}, f32[128,128]{1,0:T(8,128)S(1)}, u32[]{:S(2)}, u32[]{:S(2)}) collective-permute-start(f32[128,128]{1,0:T(8,128)S(1)} %get-tuple-element.11.refs_0_), channel_id=1, source_target_pairs={{0,4},{2,6},{4,0},{6,2},{8,12},{10,14},{12,8},{14,10},{16,20},{18,... | collective-permute-start | bytes 196616 | tf_op jit(solution)/shard_map/ppermute | solution.py:267
  11.8 5.2 %collective-permute-start.2 = (f32[128,128]{1,0:T(8,128)S(1)}, f32[128,128]{1,0:T(8,128)S(1)}, u32[]{:S(2)}, u32[]{:S(2)}) collective-permute-start(f32[128,128]{1,0:T(8,128)S(1)} %get-tuple-element.11.refs_0_), channel_id=1, source_target_pairs={{0,6},{2,4},{4,2},{6,0},{8,14},{10,12},{12,10},{14,8},{16,22},{18,... | collective-permute-start | bytes 196616 | tf_op jit(solution)/shard_map/ppermute | solution.py:267
  17.5 5.2 %collective-permute-start.3 = (f32[128,128]{1,0:T(8,128)S(1)}, f32[128,128]{1,0:T(8,128)S(1)}, u32[]{:S(2)}, u32[]{:S(2)}) collective-permute-start(f32[128,128]{1,0:T(8,128)S(1)} %shard_map.56.refs_0_), channel_id=1, source_target_pairs={{0,8},{2,10},{4,12},{6,14},{8,0},{10,2},{12,4},{14,6},{16,24},{18,... | collective-permute-start | bytes 196616 | tf_op jit(solution)/shard_map/ppermute | solution.py:267
  19.1 6.6 %collective-permute-start.4 = (f32[128,128]{1,0:T(8,128)S(1)}, f32[128,128]{1,0:T(8,128)S(1)}, u32[]{:S(2)}, u32[]{:S(2)}) collective-permute-start(f32[128,128]{1,0:T(8,128)S(1)} %shard_map.56.refs_0_), channel_id=1, source_target_pairs={{0,16},{2,18},{4,20},{6,22},{8,24},{10,26},{12,28},{14,30},{16,0},... | collective-permute-start | bytes 196616 | tf_op jit(solution)/shard_map/ppermute | solution.py:267
  21.7 6.1 %collective-permute-start.5 = (f32[128,128]{1,0:T(8,128)S(1)}, f32[128,128]{1,0:T(8,128)S(1)}, u32[]{:S(2)}, u32[]{:S(2)}) collective-permute-start(f32[128,128]{1,0:T(8,128)S(1)} %shard_map.56.refs_0_), channel_id=1, source_target_pairs={{0,24},{2,26},{4,28},{6,30},{8,16},{10,18},{12,20},{14,22},{16,8},... | collective-permute-start | bytes 196616 | tf_op jit(solution)/shard_map/ppermute | solution.py:267
  21.9 5.8 %copy-start.3 = (bf16[256,128]{1,0:T(8,128)(2,1)S(1)}, bf16[256,128]{1,0:T(8,128)(2,1)}, u32[]{:S(2)}) copy-start(bf16[256,128]{1,0:T(8,128)(2,1)} %refs_6_.1) | copy-start | bytes 196612
  42.8 2.7 %copy-start.4 = (bf16[512,64]{0,1:T(8,128)(2,1)S(1)}, bf16[512,64]{0,1:T(8,128)(2,1)}, u32[]{:S(2)}) copy-start(bf16[512,64]{0,1:T(8,128)(2,1)} %param.9) | copy-start | bytes 196612
  42.8 10.9 %all-to-all-start.1 = ((bf16[32,16,128]{2,1,0:T(8,128)(2,1)}), bf16[32,16,128]{2,1,0:T(8,128)(2,1)S(1)}, u32[]{:S(2)}, u32[]{:S(2)}) async-start(bf16[32,16,128]{2,1,0:T(8,128)(2,1)} %shard_map.60), calls=%async_computation.1 | async-start | bytes 262144 | tf_op jit(solution)/shard_map/all_to_all | solution.py:319
  45.6 1.4 %collective-permute-start.6 = (bf16[512,64]{1,0:T(8,128)(2,1)S(1)}, bf16[512,64]{1,0:T(8,128)(2,1)S(1)}, u32[]{:S(2)}, u32[]{:S(2)}) collective-permute-start(bf16[512,64]{1,0:T(8,128)(2,1)S(1)} %copy.7.refs_0_), channel_id=1, source_target_pairs={{0,1},{1,0},{2,3},{3,2},{4,5},{5,4},{6,7},{7,6},{8,9},{9,8},{10,11... | collective-permute-start | bytes 196616 | tf_op jit(solution)/shard_map/ppermute | solution.py:282

commit v3 on v2

--- a/solution.py
+++ b/solution.py
@@ -8,6 +8,7 @@
 from jax.sharding import PartitionSpec as P
 
 BLOCK = 64
+SMALL = 16
 LIMIT = 16 << 20
 F32 = jnp.float32
 BF16 = jnp.bfloat16
@@ -15,15 +16,42 @@
 SMEM = pl.BlockSpec(memory_space=pltpu.SMEM)
 
 
+def halves_of(x):
+    hi = x.astype(BF16)
+    return hi, (x - hi.astype(F32)).astype(BF16)
+
+
+def wide(x):
+    return jnp.concatenate(halves_of(x), axis=1)
+
+
+def deep(x):
+    hi, lo = halves_of(x)
+    both = jnp.concatenate([hi, lo], axis=1)
+    return jnp.concatenate([both, both], axis=0)
+
+
+def deep_nt(x):
+    hi, lo = halves_of(x)
+    return jnp.concatenate(
+        [jnp.concatenate([hi, hi], axis=1), jnp.concatenate([lo, lo], axis=1)], axis=0
+    )
+
+
+def fold(x):
+    half = x.shape[1] // 2
+    return x[:, :half] + x[:, half:]
+
+
 def mm(a, b):
-    return lax.dot_general(
-        a, b, (((1,), (0,)), ((), ())), precision=lax.Precision.HIGHEST, preferred_element_type=F32
+    return fold(
+        lax.dot_general(wide(a), deep(b), (((1,), (0,)), ((), ())), preferred_element_type=F32)
     )
 
 
 def mm_nt(a, b):
-    return lax.dot_general(
-        a, b, (((1,), (1,)), ((), ())), precision=lax.Precision.HIGHEST, preferred_element_type=F32
+    return fold(
+        lax.dot_general(wide(a), deep_nt(b), (((1,), (1,)), ((), ())), preferred_element_type=F32)
     )
 
 
@@ -65,6 +93,26 @@
     )
 
 
+def small_inverses(grams):
+    size = grams[0].shape[0]
+    count = size // SMALL
+    row, lane = iotas(SMALL, size)
+    first = lane // SMALL * SMALL
+    packs, invs = [], []
+    for gram in grams:
+        packed = jnp.zeros((SMALL, size), F32)
+        for b in range(count):
+            packed = jnp.where(lane // SMALL == b, gram[b * SMALL : (b + 1) * SMALL], packed)
+        packs.append(jnp.where(row < lane % SMALL, packed, 0.0))
+        invs.append(jnp.where(row == lane % SMALL, 1.0, 0.0))
+    for k in reversed(range(1, SMALL)):
+        columns = [jnp.take_along_axis(packed, first + k, axis=1) for packed in packs]
+        invs = [inv - column * inv[k : k + 1] for inv, column in zip(invs, columns)]
+    row, col = iotas(size, size)
+    same = row // SMALL == col // SMALL
+    return [jnp.where(same, jnp.concatenate([inv] * count, axis=0), 0.0) for inv in invs]
+
+
 def spans_kernel(raw_ref, total_ref, unit_ref, u_ref, parts_ref):
     raw = raw_ref[...].astype(F32)
     rows, width = raw.shape
@@ -72,29 +120,27 @@
     unit_ref[...] = unit
     turned = unit.T
     pair = 2 * BLOCK
+    pairs = range(rows // pair)
     row, col = iotas(pair, pair)
     ident = eye(width)
+    vs = [unit[p * pair : (p + 1) * pair] for p in pairs]
+    grams = [mm_nt(v, v) * 2.0 for v in vs]
+    size = SMALL
+    invs = small_inverses(grams)
+    while size < BLOCK:
+        corner = (row // (2 * size) == col // (2 * size)) & (row // size < col // size)
+        steps = [mm(jnp.where(corner, g, 0.0), z) for g, z in zip(grams, invs)]
+        invs = [z - mm(z, t) for z, t in zip(invs, steps)]
+        size *= 2
+    us = [mm(z, v) * 2.0 for z, v in zip(invs, vs)]
     blocks = []
-    for p in range(rows // pair):
-        v = unit[p * pair : (p + 1) * pair]
-        gram = mm_nt(v, v) * 2.0
-        size = 1
-        inv = jnp.where(row == col, 1.0, 0.0)
-        while size < BLOCK:
-            corner = (row // (2 * size) == col // (2 * size)) & (row // size < col // size)
-            c = jnp.where(corner, gram, 0.0)
-            if size == 1:
-                inv = inv - c
-            else:
-                inv = inv - mm(inv, mm(c, inv))
-            size *= 2
-        u = mm(inv, v) * 2.0
-        u_ref[p * pair : (p + 1) * pair, :] = u
+    for p in pairs:
+        u_ref[p * pair : (p + 1) * pair, :] = us[p]
         for b in range(2):
             lo = p * pair + b * BLOCK
-            q = ident - mm(turned[:, lo : lo + BLOCK], u[b * BLOCK : (b + 1) * BLOCK])
-            parts_ref[2 * p + b] = q
-            blocks.append(q)
+            blocks.append(ident - mm(turned[:, lo : lo + BLOCK], us[p][b * BLOCK : (b + 1) * BLOCK]))
+    for b, q in enumerate(blocks):
+        parts_ref[b] = q
     total_ref[...] = chain(blocks)
 
 

time: 55.1 us -> 49 us (0.89)
  Pallas kernels: 15 us -> 8.62 us
    pallas_call x1, Pallas kernels: 6.33 us -> 1.9 us  [on_device(): call(spans_kernel, [square, tall, tall, jax.ShapeDtypeStruct((blocks, wid...]
    pallas_call x1, Pallas kernels: 3.27 us -> 1.8 us  [on_device(): call(functools.partial(attend_kernel, stride, radix, heads), jax.ShapeDty...]
where the time goes in v3:
time: 49 us; the launch traced here: 48.7 us
  waiting for transfers between devices  16.6 us (34%)
  starting transfers between devices  11.9 us (24%)
  blocking collectives  10.5 us (21%)
  Pallas kernels  8.62 us (18%)
  local copies, waits for them, and re-layouts  1.01 us (2%)
    all_to_all x1, blocking collectives, on_device(): lax.all_to_all(packed, 'seq', split_axis=0, concat_axis=0, tiled=True)  10.5 us
    ppermute x6, starting transfers between devices, exchange(): got.append(lax.ppermute(x, 'seq', pairs))  9.03 us
    ppermute x6, waiting for transfers between devices, exchange(): got.append(lax.ppermute(x, 'seq', pairs))  8.72 us
    all_to_all x1, waiting for transfers between devices, on_device(): lax.all_to_all(spread, ('seq', 'head'), split_axis=0, concat_axis=0, tile...  6.66 us
    all_to_all x1, starting transfers between devices, on_device(): lax.all_to_all(spread, ('seq', 'head'), split_axis=0, concat_axis=0, tile...  2.69 us
    pallas_call x1, Pallas kernels, on_device(): call(spans_kernel, [square, tall, tall, jax.ShapeDtypeStruct((blocks, wid...  1.9 us
    pallas_call x1, Pallas kernels, on_device(): call(functools.partial(attend_kernel, stride, radix, heads), jax.ShapeDty...  1.8 us
    pallas_call x1, Pallas kernels, on_device(): call(functools.partial(carry_kernel, parts), [tall, jax.ShapeDtypeStruct(...  1.7 us
  transfers between devices with their start and end apart: 8, of which 6 were waited for; matrix products, arithmetic and copies ran while one was open for 0% of the time, Pallas kernels for 5%

profile of v3, /device:TPU:0, one launch (start us, length us, event | category | flops | bytes accessed | tf_op | source)
XLA Modules:
  0.0 48.7 jit_solution(18019279761830849289)
XLA Ops:
  0.0 0.0 copy-start
  0.0 0.0 copy-start.1
  0.0 0.9 %copy-done.1 = bf16[256,128]{1,0:T(8,128)(2,1)S(1)} copy-done((bf16[256,128]{1,0:T(8,128)(2,1)S(1)}, bf16[256,128]{1,0:T(8,128)(2,1)}, u32[]{:S(2)}) %copy-start.1) | copy-done | bytes 65560
  0.9 0.0 copy-start.2
  0.9 1.9 %shard_map.55 = (f32[128,128]{1,0:T(8,128)S(1)}, f32[256,128]{1,0:T(8,128)S(1)}, f32[256,128]{1,0:T(8,128)S(1)}, f32[4,128,128]{2,1,0:T(8,128)S(1)}) custom-call(bf16[256,128]{1,0:T(8,128)(2,1)S(1)} %copy-done.1), custom_call_target="tpu_custom_call" | custom-call | flops 1073741824 | bytes 1048576 | tf_op jit(solution)/shard_map/pallas_call | solution.py:329
  2.8 3.0 %collective-permute-start = (f32[128,128]{1,0:T(8,128)S(1)}, f32[128,128]{1,0:T(8,128)S(1)}, u32[]{:S(2)}, u32[]{:S(2)}) collective-permute-start(f32[128,128]{1,0:T(8,128)S(1)} %get-tuple-element.11.refs_0_), channel_id=1, source_target_pairs={{0,2},{2,0},{4,6},{6,4},{8,10},{10,8},{12,14},{14,12},{16,18},{18,... | collective-permute-start | bytes 196616 | tf_op jit(solution)/shard_map/ppermute | solution.py:313
  5.8 1.5 %collective-permute-start.1 = (f32[128,128]{1,0:T(8,128)S(1)}, f32[128,128]{1,0:T(8,128)S(1)}, u32[]{:S(2)}, u32[]{:S(2)}) collective-permute-start(f32[128,128]{1,0:T(8,128)S(1)} %get-tuple-element.11.refs_0_), channel_id=1, source_target_pairs={{0,4},{2,6},{4,0},{6,2},{8,12},{10,14},{12,8},{14,10},{16,20},{18,... | collective-permute-start | bytes 196616 | tf_op jit(solution)/shard_map/ppermute | solution.py:313
  7.3 0.0 collective-permute-start.2
  7.4 0.0 copy-done
  7.4 0.0 copy-done.2
  7.4 1.7 %shard_map.57 = (f32[256,128]{1,0:T(8,128)S(1)}, bf16[128,512]{1,0:T(8,128)(2,1)S(1)}) custom-call(bf16[256,128]{1,0:T(8,128)(2,1)S(1)} %copy-done.2, f32[256,128]{1,0:T(8,128)S(1)} %get-tuple-element.12.unit_ref, f32[256,128]{1,0:T(8,128)S(1)} %get-tuple-element.13.u_ref, f32[4,128,128]{2,1,0:T(8,128)S(1)} %get-tuple-element.14.parts_ref, ...), custom_call_target="tpu_custom_call" | custom-call | flops 2147483648 | bytes 1048576 | tf_op jit(solution)/shard_map/pallas_call | solution.py:343
  9.1 0.0 collective-permute-done.refs_1_
  9.1 1.0 %collective-permute-done.1.refs_2_ = f32[128,128]{1,0:T(8,128)S(1)} collective-permute-done((f32[128,128]{1,0:T(8,128)S(1)}, f32[128,128]{1,0:T(8,128)S(1)}, u32[]{:S(2)}, u32[]{:S(2)}) %collective-permute-start.1) | collective-permute-done | bytes 65568 | tf_op jit(solution)/shard_map/ppermute | solution.py:313
  10.1 2.4 %collective-permute-done.2.refs_3_ = f32[128,128]{1,0:T(8,128)S(1)} collective-permute-done((f32[128,128]{1,0:T(8,128)S(1)}, f32[128,128]{1,0:T(8,128)S(1)}, u32[]{:S(2)}, u32[]{:S(2)}) %collective-permute-start.2) | collective-permute-done | bytes 65568 | tf_op jit(solution)/shard_map/ppermute | solution.py:313
  12.5 0.4 shard_map.56.refs_0_
  12.9 1.6 %collective-permute-start.3 = (f32[128,128]{1,0:T(8,128)S(1)}, f32[128,128]{1,0:T(8,128)S(1)}, u32[]{:S(2)}, u32[]{:S(2)}) collective-permute-start(f32[128,128]{1,0:T(8,128)S(1)} %shard_map.56.refs_0_), channel_id=1, source_target_pairs={{0,8},{2,10},{4,12},{6,14},{8,0},{10,2},{12,4},{14,6},{16,24},{18,... | collective-permute-start | bytes 196616 | tf_op jit(solution)/shard_map/ppermute | solution.py:313
  14.5 2.6 %collective-permute-start.4 = (f32[128,128]{1,0:T(8,128)S(1)}, f32[128,128]{1,0:T(8,128)S(1)}, u32[]{:S(2)}, u32[]{:S(2)}) collective-permute-start(f32[128,128]{1,0:T(8,128)S(1)} %shard_map.56.refs_0_), channel_id=1, source_target_pairs={{0,16},{2,18},{4,20},{6,22},{8,24},{10,26},{12,28},{14,30},{16,0},... | collective-permute-start | bytes 196616 | tf_op jit(solution)/shard_map/ppermute | solution.py:313
  17.1 0.2 collective-permute-start.5
  17.3 0.0 copy-start.3
  17.3 0.5 %shard_map.58.refs_4_ = f32[256,128]{1,0:T(8,128)S(1)} custom-call(f32[128,128]{1,0:T(8,128)S(1)} %get-tuple-element.11.refs_0_, f32[128,128]{1,0:T(8,128)S(1)} %collective-permute-done.refs_1_, f32[128,128]{1,0:T(8,128)S(1)} %collective-permute-done.1.refs_2_, f32[128,128]{1,0:T(8,128)S(1)} %collective-permute-done.2.refs_3_, ...), custom_call_target="tpu_custom_call" | custom-call | flops 1073741824 | bytes 1048576 | tf_op jit(solution)/shard_map/pallas_call | solution.py:350
  17.9 0.0 collective-permute-done.3.refs_1_
  17.9 3.2 %collective-permute-done.4.refs_2_ = f32[128,128]{1,0:T(8,128)S(1)} collective-permute-done((f32[128,128]{1,0:T(8,128)S(1)}, f32[128,128]{1,0:T(8,128)S(1)}, u32[]{:S(2)}, u32[]{:S(2)}) %collective-permute-start.4) | collective-permute-done | bytes 65568 | tf_op jit(solution)/shard_map/ppermute | solution.py:313
  21.1 2.1 %collective-permute-done.5.refs_3_ = f32[128,128]{1,0:T(8,128)S(1)} collective-permute-done((f32[128,128]{1,0:T(8,128)S(1)}, f32[128,128]{1,0:T(8,128)S(1)}, u32[]{:S(2)}, u32[]{:S(2)}) %collective-permute-start.5) | collective-permute-done | bytes 65568 | tf_op jit(solution)/shard_map/ppermute | solution.py:313
  23.2 0.0 copy-done.3
  23.2 1.8 %shard_map.59 = bf16[16,8,640]{2,1,0:T(8,128)(2,1)S(1)} custom-call(f32[128,128]{1,0:T(8,128)S(1)} %shard_map.56.refs_0_, f32[128,128]{1,0:T(8,128)S(1)} %collective-permute-done.3.refs_1_, f32[128,128]{1,0:T(8,128)S(1)} %collective-permute-done.4.refs_2_, f32[128,128]{1,0:T(8,128)S(1)} %collective-permute-done.5.refs_3_, f32[256,128]{1,0:T(8,128)S(1)} %shard_map.58.refs_4_, ...), custom_call_target="tpu_custom_call" | custom-call | flops 2147483648 | bytes 1048576 | tf_op jit(solution)/shard_map/pallas_call | solution.py:353
  25.0 10.5 %all_to_all.10.got_ref = bf16[16,8,640]{2,1,0:T(8,128)(2,1)S(1)} all-to-all(bf16[16,8,640]{2,1,0:T(8,128)(2,1)S(1)} %shard_map.59), channel_id=1, replica_groups=mesh['seq'=16,'head'=2] {'seq'}, dimensions={0} | all-to-all | bytes 327680 | tf_op jit(solution)/shard_map/all_to_all | solution.py:358
  35.5 1.2 %shard_map.60 = bf16[32,16,128]{2,1,0:T(8,128)(2,1)} custom-call(bf16[16,8,640]{2,1,0:T(8,128)(2,1)S(1)} %all_to_all.10.got_ref), custom_call_target="tpu_custom_call" | custom-call | flops 67108864 | bytes 1048576 | tf_op jit(solution)/shard_map/pallas_call | solution.py:360
  36.7 0.0 copy-start.4
  36.7 2.7 %all-to-all-start.1 = ((bf16[32,16,128]{2,1,0:T(8,128)(2,1)}), bf16[32,16,128]{2,1,0:T(8,128)(2,1)S(1)}, u32[]{:S(2)}, u32[]{:S(2)}) async-start(bf16[32,16,128]{2,1,0:T(8,128)(2,1)} %shard_map.60), calls=%async_computation.1 | async-start | bytes 262144 | tf_op jit(solution)/shard_map/all_to_all | solution.py:365
  39.4 0.0 copy-done.4
  39.4 0.1 copy.7.refs_0_
  39.5 0.2 collective-permute-start.6
  39.7 1.2 %collective-permute-done.6.refs_1_ = bf16[512,64]{1,0:T(8,128)(2,1)S(1)} collective-permute-done((bf16[512,64]{1,0:T(8,128)(2,1)S(1)}, bf16[512,64]{1,0:T(8,128)(2,1)S(1)}, u32[]{:S(2)}, u32[]{:S(2)}) %collective-permute-start.6) | collective-permute-done | bytes 65568 | tf_op jit(solution)/shard_map/ppermute | solution.py:328
  41.0 6.7 %all-to-all-done.1.got_ref = bf16[32,16,128]{2,1,0:T(8,128)(2,1)S(1)} async-done(((bf16[32,16,128]{2,1,0:T(8,128)(2,1)}), bf16[32,16,128]{2,1,0:T(8,128)(2,1)S(1)}, u32[]{:S(2)}, u32[]{:S(2)}) %all-to-all-start.1) | async-done | bytes 131104 | tf_op jit(solution)/shard_map/all_to_all | solution.py:365
  47.6 1.1 %shard_map.61 = bf16[64,64]{1,0:T(8,128)(2,1)} custom-call(bf16[32,16,128]{2,1,0:T(8,128)(2,1)S(1)} %all-to-all-done.1.got_ref, bf16[512,64]{1,0:T(8,128)(2,1)S(1)} %copy.7.refs_0_, bf16[512,64]{1,0:T(8,128)(2,1)S(1)} %collective-permute-done.6.refs_1_), custom_call_target="tpu_custom_call" | custom-call | flops 268435456 | bytes 1048576 | tf_op jit(solution)/shard_map/pallas_call | solution.py:366
Async XLA Ops:
  0.0 7.4 %copy-start = (bf16[128,512]{1,0:T(8,128)(2,1)S(1)}, bf16[128,512]{1,0:T(8,128)(2,1)}, u32[]{:S(2)}) copy-start(bf16[128,512]{1,0:T(8,128)(2,1)} %queries_ref.1) | copy-start | bytes 393220
  0.0 0.9 %copy-start.1 = (bf16[256,128]{1,0:T(8,128)(2,1)S(1)}, bf16[256,128]{1,0:T(8,128)(2,1)}, u32[]{:S(2)}) copy-start(bf16[256,128]{1,0:T(8,128)(2,1)} %raw_ref.1) | copy-start | bytes 196612
  0.9 6.5 %copy-start.2 = (bf16[256,128]{1,0:T(8,128)(2,1)S(1)}, bf16[256,128]{1,0:T(8,128)(2,1)}, u32[]{:S(2)}) copy-start(bf16[256,128]{1,0:T(8,128)(2,1)} %keys_ref.1) | copy-start | bytes 196612
  2.8 6.3 %collective-permute-start = (f32[128,128]{1,0:T(8,128)S(1)}, f32[128,128]{1,0:T(8,128)S(1)}, u32[]{:S(2)}, u32[]{:S(2)}) collective-permute-start(f32[128,128]{1,0:T(8,128)S(1)} %get-tuple-element.11.refs_0_), channel_id=1, source_target_pairs={{0,2},{2,0},{4,6},{6,4},{8,10},{10,8},{12,14},{14,12},{16,18},{18,... | collective-permute-start | bytes 196616 | tf_op jit(solution)/shard_map/ppermute | solution.py:313
  5.8 4.3 %collective-permute-start.1 = (f32[128,128]{1,0:T(8,128)S(1)}, f32[128,128]{1,0:T(8,128)S(1)}, u32[]{:S(2)}, u32[]{:S(2)}) collective-permute-start(f32[128,128]{1,0:T(8,128)S(1)} %get-tuple-element.11.refs_0_), channel_id=1, source_target_pairs={{0,4},{2,6},{4,0},{6,2},{8,12},{10,14},{12,8},{14,10},{16,20},{18,... | collective-permute-start | bytes 196616 | tf_op jit(solution)/shard_map/ppermute | solution.py:313
  7.3 5.2 %collective-permute-start.2 = (f32[128,128]{1,0:T(8,128)S(1)}, f32[128,128]{1,0:T(8,128)S(1)}, u32[]{:S(2)}, u32[]{:S(2)}) collective-permute-start(f32[128,128]{1,0:T(8,128)S(1)} %get-tuple-element.11.refs_0_), channel_id=1, source_target_pairs={{0,6},{2,4},{4,2},{6,0},{8,14},{10,12},{12,10},{14,8},{16,22},{18,... | collective-permute-start | bytes 196616 | tf_op jit(solution)/shard_map/ppermute | solution.py:313
  12.9 5.0 %collective-permute-start.3 = (f32[128,128]{1,0:T(8,128)S(1)}, f32[128,128]{1,0:T(8,128)S(1)}, u32[]{:S(2)}, u32[]{:S(2)}) collective-permute-start(f32[128,128]{1,0:T(8,128)S(1)} %shard_map.56.refs_0_), channel_id=1, source_target_pairs={{0,8},{2,10},{4,12},{6,14},{8,0},{10,2},{12,4},{14,6},{16,24},{18,... | collective-permute-start | bytes 196616 | tf_op jit(solution)/shard_map/ppermute | solution.py:313
  14.5 6.6 %collective-permute-start.4 = (f32[128,128]{1,0:T(8,128)S(1)}, f32[128,128]{1,0:T(8,128)S(1)}, u32[]{:S(2)}, u32[]{:S(2)}) collective-permute-start(f32[128,128]{1,0:T(8,128)S(1)} %shard_map.56.refs_0_), channel_id=1, source_target_pairs={{0,16},{2,18},{4,20},{6,22},{8,24},{10,26},{12,28},{14,30},{16,0},... | collective-permute-start | bytes 196616 | tf_op jit(solution)/shard_map/ppermute | solution.py:313
  17.1 6.1 %collective-permute-start.5 = (f32[128,128]{1,0:T(8,128)S(1)}, f32[128,128]{1,0:T(8,128)S(1)}, u32[]{:S(2)}, u32[]{:S(2)}) collective-permute-start(f32[128,128]{1,0:T(8,128)S(1)} %shard_map.56.refs_0_), channel_id=1, source_target_pairs={{0,24},{2,26},{4,28},{6,30},{8,16},{10,18},{12,20},{14,22},{16,8},... | collective-permute-start | bytes 196616 | tf_op jit(solution)/shard_map/ppermute | solution.py:313
  17.3 5.8 %copy-start.3 = (bf16[256,128]{1,0:T(8,128)(2,1)S(1)}, bf16[256,128]{1,0:T(8,128)(2,1)}, u32[]{:S(2)}) copy-start(bf16[256,128]{1,0:T(8,128)(2,1)} %refs_6_.1) | copy-start | bytes 196612
  36.7 2.7 %copy-start.4 = (bf16[512,64]{0,1:T(8,128)(2,1)S(1)}, bf16[512,64]{0,1:T(8,128)(2,1)}, u32[]{:S(2)}) copy-start(bf16[512,64]{0,1:T(8,128)(2,1)} %param.9) | copy-start | bytes 196612
  36.7 10.9 %all-to-all-start.1 = ((bf16[32,16,128]{2,1,0:T(8,128)(2,1)}), bf16[32,16,128]{2,1,0:T(8,128)(2,1)S(1)}, u32[]{:S(2)}, u32[]{:S(2)}) async-start(bf16[32,16,128]{2,1,0:T(8,128)(2,1)} %shard_map.60), calls=%async_computation.1 | async-start | bytes 262144 | tf_op jit(solution)/shard_map/all_to_all | solution.py:365
  39.5 1.4 %collective-permute-start.6 = (bf16[512,64]{1,0:T(8,128)(2,1)S(1)}, bf16[512,64]{1,0:T(8,128)(2,1)S(1)}, u32[]{:S(2)}, u32[]{:S(2)}) collective-permute-start(bf16[512,64]{1,0:T(8,128)(2,1)S(1)} %copy.7.refs_0_), channel_id=1, source_target_pairs={{0,1},{1,0},{2,3},{3,2},{4,5},{5,4},{6,7},{7,6},{8,9},{9,8},{10,11... | collective-permute-start | bytes 196616 | tf_op jit(solution)/shard_map/ppermute | solution.py:328
